TPU v7x, 256 devices: a whole 4x4x8 slice. The times are simulated.
256 devices in a mesh: leaf: 64 (over x, z, core), rhs: 4 (over y).
Axes of the slice: x: 4, y: 4, z: 8, core: 2. Of those that a mesh axis runs over, the one named last changes fastest.
Arguments:
- input_columns: float32 [8, 1024, 256], P('rhs', 'leaf'), may hold values from -6 to 6
- near_blocks: float32 [8192, 256, 256], P(('leaf', 'rhs')), may hold values from -0.25 to 0.25
- near_pairs: int32 [8192, 2], P(('leaf', 'rhs')), may hold values from -1 to 1023, as said below
- leaf_basis: float32 [1024, 64, 256], P(('leaf', 'rhs')), may hold values from -0.375 to 0.375
- local_transfer: float32 [1792, 64, 64], P('leaf'), may hold values from -0.5 to 0.5
- local_coupling: float32 [1792, 4, 64, 64], P('leaf'), may hold values from -0.4375 to 0.4375
- local_lists: int32 [1792, 4], P('leaf'), may hold values from -1 to 1023, as said below
- middle_transfer: float32 [128, 64, 64], P('leaf'), may hold values from -0.5 to 0.5
- middle_coupling: float32 [192, 4, 64, 64], P('leaf'), may hold values from -0.75 to 0.75
- middle_lists: int32 [192, 4], P('leaf'), may hold values from -1 to 127, as said below
- upper_transfer: float32 [126, 64, 64], replicated, may hold values from -0.5 to 0.5
- upper_coupling: float32 [64, 4, 64, 64], P('leaf'), may hold values from -1 to 1
- upper_lists: int32 [64, 4], P('leaf'), may hold values from -1 to 31, as said below
Outputs:
- first_product: float32 [8, 1024, 256], P(None, ('leaf', 'rhs'))
- second_product: float32 [8, 1024, 256], P(None, ('leaf', 'rhs'))
Inputs may be any that keep to these rules, and one draw needn't show every extreme that they name: `near_pairs`: each slot holds (receiving leaf, source leaf). The 32 slots of each device along leaf+rhs belong to receiving leaves among that device's 4 leaves; live pairs come first, the remaining slots are -1 in both columns. The source leaf lies within 4 leaves of the receiving one. In every draw some device has all its slots live. `local_lists`: each entry is -1 (unused) or the number, among the clusters of the same level counted from 0 in leaf order, of a cluster whose number differs from the listing cluster's by 2 or 3; entries of one list differ. `middle_lists`: as for the local lists, at the level of the subtree roots and the level below it. `upper_lists`: row h lists for heap cluster h (level t with 2^t <= h < 2^(t+1), number h - 2^t) as for the local lists; rows 0 to 3 are -1.
All inputs are finite; a program needn't handle non-finite values.
Results may differ from a plain program's by a relative error of at most 0.0003.
Values sent between devices are 32-bit elements; how exact they have to be, the bound alone decides.
A program may use at most 128 MiB of HBM per device.

v0:
```python
import jax
import jax.numpy as jnp
from jax import lax
from jax.sharding import PartitionSpec as P

NEAR_REACH = 4


highest = lax.Precision.HIGHEST


def with_halo(shard, sides, width):
    for axis, dim in sides:
        count, length = (lax.axis_size(axis), shard.shape[dim])
        up = [(i, (i + 1) % count) for i in range(count - 1)]
        down = [(j, i) for i, j in up]
        last = lax.slice_in_dim(shard, length - width, length, axis=dim)
        leading = lax.slice_in_dim(shard, 0, width, axis=dim)
        before = lax.ppermute(last, axis, up)
        after = lax.ppermute(leading, axis, down)
        shard = jnp.concatenate([before, shard, after], axis=dim)
    return shard


def lift_level(matrices, vectors):
    moved = jnp.einsum("nab,cna->cnb", matrices, vectors, precision=highest)
    return moved.reshape(moved.shape[0], moved.shape[1] // 2, 2, moved.shape[2]).sum(axis=2)


def couple_lists(blocks, positions, valid, table):
    clipped = jnp.clip(positions, 0, table.shape[1] - 1)
    picked = jnp.take(table, clipped, axis=1)
    picked = picked * valid.astype(table.dtype)[None, :, :, None]
    return jnp.einsum("nkab,cnkb->cna", blocks, picked, precision=highest)


def near_field(vectors_rows, near_blocks, near_pairs, first_leaf):
    extended = with_halo(vectors_rows, ((("leaf", "rhs"), 1),), NEAR_REACH)
    leaf_share = vectors_rows.shape[1]
    sources = jnp.clip(near_pairs[:, 1] - first_leaf + NEAR_REACH, 0, extended.shape[1] - 1)
    picked = jnp.take(extended, sources, axis=1)
    terms = jnp.einsum("pij,rpj->rpi", near_blocks, picked, precision=highest)
    targets = near_pairs[:, 0] - first_leaf
    owners = (targets[None, :] == jnp.arange(leaf_share, dtype=jnp.int32)[:, None]).astype(
        jnp.float32
    )
    return jnp.einsum("lp,rpi->rli", owners, terms, precision=highest)


def tree_pass(leaf_coeffs, group, groups, tree_data):
    (
        local_transfer,
        local_coupling,
        local_lists,
        middle_transfer,
        middle_coupling,
        middle_lists,
        upper_transfer,
        upper_coupling,
        upper_lists,
    ) = tree_data
    leaf_total = leaf_coeffs.shape[1]
    local_levels = leaf_total.bit_length() - 2
    top_depth = groups.bit_length() - 1
    amounts = [4 * 2**sublevel for sublevel in range(local_levels)]
    offsets = [4 * (2**sublevel - 1) for sublevel in range(local_levels)]
    upward = [leaf_coeffs] * local_levels
    for sublevel in range(local_levels - 1, 0, -1):
        start_row = offsets[sublevel]
        upward[sublevel - 1] = lift_level(
            local_transfer[start_row : start_row + amounts[sublevel]], upward[sublevel]
        )
    upper_pair = lift_level(local_transfer[0:4], upward[0])
    subtree_root = lift_level(middle_transfer, upper_pair)
    rims = jnp.stack(
        [
            jnp.concatenate([level_coeffs[:, :3], level_coeffs[:, -3:]], axis=1)
            for level_coeffs in upward
        ],
        axis=1,
    )
    bordered = with_halo(rims, (("leaf", 2),), 3)
    all_roots, all_pairs = (
        lax.all_gather(subtree_root, "leaf", axis=1, tiled=True),
        lax.all_gather(upper_pair, "leaf", axis=1, tiled=True),
    )
    climbing = {top_depth: all_roots}
    for tree_level in range(top_depth, 0, -1):
        lower_end = 2**tree_level
        climbing[tree_level - 1] = lift_level(
            upper_transfer[lower_end - 2 : 2 * lower_end - 2], climbing[tree_level]
        )
    numbered = jnp.concatenate(
        [jnp.zeros_like(climbing[0])] + [climbing[tree_level] for tree_level in range(top_depth)],
        axis=1,
    )
    level_start = jnp.int32(1)
    for exponent in range(1, top_depth):
        level_start = jnp.where(group >= 2**exponent, 2**exponent, level_start)
    owned_terms = couple_lists(
        upper_coupling, upper_lists + level_start, upper_lists >= 0, numbered
    )
    ancestor = lax.all_gather(owned_terms, "leaf", axis=1, tiled=True)
    descending = jnp.zeros_like(owned_terms[:, 0])
    for tree_level in range(1, top_depth):
        node_index = 2**tree_level + group // 2 ** (top_depth - tree_level)
        matrix = lax.dynamic_index_in_dim(upper_transfer, node_index - 2, 0, keepdims=False)
        descending = lax.dynamic_index_in_dim(ancestor, node_index, 1, keepdims=False) + jnp.einsum(
            "ab,cb->ca", matrix, descending, precision=highest
        )
    root_matrix = lax.dynamic_index_in_dim(upper_transfer, groups - 2 + group, 0, keepdims=False)
    root_lists = middle_lists[0:1]
    root_down = couple_lists(middle_coupling[0:1], root_lists, root_lists >= 0, all_roots)[
        :, 0
    ] + jnp.einsum("ab,cb->ca", root_matrix, descending, precision=highest)
    pair_lists = middle_lists[1:3]
    descending = couple_lists(
        middle_coupling[1:3], pair_lists, pair_lists >= 0, all_pairs
    ) + jnp.einsum("nab,cb->cna", middle_transfer, root_down, precision=highest)
    for sublevel in range(local_levels):
        amount = amounts[sublevel]
        offset = offsets[sublevel]
        extended = jnp.concatenate(
            [bordered[:, sublevel, :3], upward[sublevel], bordered[:, sublevel, 9:]], axis=1
        )
        entries = local_lists[offset : offset + amount]
        coupled = couple_lists(
            local_coupling[offset : offset + amount],
            entries - group * amount + 3,
            entries >= 0,
            extended,
        )
        descending = coupled + jnp.einsum(
            "nab,cnb->cna",
            local_transfer[offset : offset + amount],
            jnp.repeat(descending, 2, axis=1),
            precision=highest,
        )
    return descending


def apply_matrix(vectors_rows, near_blocks, near_pairs, leaf_basis, tree_data):
    group = lax.axis_index("leaf")
    groups = lax.axis_size("leaf")
    quarter = lax.axis_index("rhs")
    quarters = lax.axis_size("rhs")
    leaf_share = vectors_rows.shape[1]
    first_leaf = (group * quarters + quarter) * leaf_share
    near_part = near_field(vectors_rows, near_blocks, near_pairs, first_leaf)
    own_coeffs = jnp.einsum("lki,rli->rlk", leaf_basis, vectors_rows, precision=highest)
    leaf_coeffs = lax.all_gather(own_coeffs, "rhs", axis=1, tiled=True)
    descending = tree_pass(leaf_coeffs, group, groups, tree_data)
    own_rows = lax.dynamic_slice_in_dim(descending, quarter * leaf_share, leaf_share, 1)
    far_part = jnp.einsum("lki,rlk->rli", leaf_basis, own_rows, precision=highest)
    return near_part + far_part


def body(
    input_columns,
    near_blocks,
    near_pairs,
    leaf_basis,
    local_transfer,
    local_coupling,
    local_lists,
    middle_transfer,
    middle_coupling,
    middle_lists,
    upper_transfer,
    upper_coupling,
    upper_lists,
):
    tree_data = (
        local_transfer,
        local_coupling,
        local_lists,
        middle_transfer,
        middle_coupling,
        middle_lists,
        upper_transfer,
        upper_coupling,
        upper_lists,
    )
    vectors_rows = lax.all_to_all(input_columns, "rhs", split_axis=1, concat_axis=0, tiled=True)
    first_product = apply_matrix(vectors_rows, near_blocks, near_pairs, leaf_basis, tree_data)
    second_product = apply_matrix(first_product, near_blocks, near_pairs, leaf_basis, tree_data)
    return (first_product, second_product)


def solution(mesh):
    in_specs = (
        P("rhs", "leaf", None),
        P(("leaf", "rhs"), None, None),
        P(("leaf", "rhs"), None),
        P(("leaf", "rhs"), None, None),
        P("leaf", None, None),
        P("leaf", None, None, None),
        P("leaf", None),
        P("leaf", None, None),
        P("leaf", None, None, None),
        P("leaf", None),
        P(),
        P("leaf", None, None, None),
        P("leaf", None),
    )
    out_specs = (P(None, ("leaf", "rhs"), None), P(None, ("leaf", "rhs"), None))
    return jax.shard_map(body, mesh=mesh, in_specs=in_specs, out_specs=out_specs, check_vma=False)
```

profile of v0, /device:TPU:1, one launch (start us, length us, event | category | flops | bytes accessed | tf_op | source)
XLA Modules:
  0.0 549.1 jit_solution(10016394474385720229)
XLA Ops:
  0.6 1.4 copy.124
  2.1 5.0 all-to-all-start
  15.4 13.1 %constant_dynamic-slice_fusion.5 = (f32[1,64,64]{0,2,1:T(8,128)}, f32[1,64,64]{0,2,1:T(8,128)}, f32[1,64,64]{0,2,1:T(8,128)}, f32[1,64,64]{0,2,1:T(8,128)}, f32[1,64,64]{0,2,1:T(8,128)}, /*index=5*/f32[1,64,64]{0,2,1:T(8,128)}) fusion(f32[126,64,64]{0,2,1:T(8,128)} %param.35, s32[]{:T(128)S(6)} %select_n.163, s32[]{:T(128)S(6)} %select_n.162, ...), kind=kLoop, calls=%fused_computation.260 | loop fusion | bytes 196632 | tf_op jit(solution)/shard_map/jit(dynamic_index_in_dim)/dynamic_slice | solution.py:111
  28.5 2.4 copy.181
  36.4 2.0 slice.203
  38.4 1.9 slice.204
  40.3 1.9 slice.205
  42.2 1.9 slice.206
  44.2 1.9 slice.207
  46.1 4.3 copy.175
  50.4 3.4 copy.176
  53.7 3.0 copy.177
  56.8 2.2 copy.178
  59.0 2.9 copy.179
  63.2 3.0 copy.182
  67.5 3.0 copy.184
  70.6 2.9 copy.185
  82.6 9.6 %all_gather.24 = f32[8,16,64]{2,0,1:T(8,128)S(1)} all-gather(f32[8,4,64]{2,0,1:T(8,128)S(1)} %convolution_bitcast_fusion.7), channel_id=1, replica_groups=mesh['leaf'=64,'rhs'=4] {'rhs'}, dimensions={1}, use_global_device_ids=true | all-gather | bytes 40960 | tf_op jit(solution)/shard_map/all_gather | solution.py:151
  95.1 3.1 collective-permute-start
  98.2 7.9 %collective-permute-start.1 = (f32[8,4,256]{2,0,1:T(8,128)}, f32[8,4,256]{2,0,1:T(8,128)}, u32[]{:S(2)}, u32[]{:S(2)}) collective-permute-start(f32[8,4,256]{2,0,1:T(8,128)} %all_to_all.16), channel_id=1, source_target_pairs={{1,0},{2,1},{3,2},{4,3},{5,4},{6,5},{7,6},{8,7},{9,8},{10,9},{11,1... | collective-permute-start | bytes 98312 | tf_op jit(solution)/shard_map/ppermute | solution.py:20
  106.2 58.5 %all_gather.25 = f32[8,128,64]{2,0,1:T(8,128)} all-gather(f32[8,2,64]{2,0,1:T(8,128)S(1)} %bitcast_reduce_fusion.15), channel_id=1, replica_groups=mesh['leaf'=64,'rhs'=4] {'leaf'}, dimensions={1}, use_global_device_ids=true | all-gather | bytes 266240 | tf_op jit(solution)/shard_map/all_gather | solution.py:85
  165.8 43.2 %all-gather.4 = f32[64,64,8]{1,2,0:T(8,128)S(1)} all-gather(f32[1,64,8]{1,2,0:T(8,128)S(1)} %convolution_bitcast_fusion.19), channel_id=2, replica_groups=mesh['leaf'=64,'rhs'=4] {'leaf'}, dimensions={0}, use_global_device_ids=true | all-gather | bytes 133120 | tf_op jit(solution)/shard_map/all_gather | solution.py:84
  209.7 1.7 reshape.343
  211.4 1.7 reshape.316
  213.2 1.9 copy.137
  215.1 2.9 bitcast_reduce_fusion.1
  221.0 2.2 gather_fusion.6
  224.4 42.1 %all-gather.5 = f32[64,64,8]{1,2,0:T(8,128)S(1)} all-gather(f32[1,64,8]{1,2,0:T(8,128)S(1)} %convolution_bitcast_fusion.16), channel_id=3, replica_groups=mesh['leaf'=64,'rhs'=4] {'leaf'}, dimensions={0}, use_global_device_ids=true | all-gather | bytes 133120 | tf_op jit(solution)/shard_map/all_gather | solution.py:103
  267.2 1.7 reshape.345
  268.9 1.7 reshape.317
  272.8 2.5 collective-permute-start.2
  275.3 2.6 collective-permute-start.3
  277.9 2.2 gather_fusion.5
  280.1 2.3 gather_fusion.4
  289.1 1.4 convolution_bitcast_fusion.11
  290.5 1.7 convolution_add_fusion.5
  295.5 2.1 gather_fusion.3
  297.6 1.7 convolution_bitcast_fusion.9
  300.9 1.4 pad_maximum_fusion.6
  302.3 2.2 gather_fusion.2
  304.5 2.3 convolution_bitcast_fusion.4
  308.1 1.6 fusion.28
  310.3 2.3 gather_fusion.1
  312.6 3.6 fusion.4
  316.2 1.6 fusion.106
  317.8 1.4 pad_maximum_fusion.1
  319.2 2.3 gather_fusion
  321.5 10.5 %convolution_bitcast_fusion.1 = f32[8,32,256]{2,0,1:T(8,128)S(1)} fusion(f32[32,256,256]{2,1,0:T(8,128)} %param.26, f32[32,8,256]{2,1,0:T(8,128)} %gather_fusion, pred[32]{0:T(512)(128)(4,1)S(1)} %copy-done.55), kind=kOutput, calls=%fused_computation.19 | convolution fusion | flops 201392128 | bytes 8912928 | tf_op jit(solution)/shard_map/pij,rpj->rpi/dot_general | solution.py:42
  333.9 9.6 %all_gather.28 = f32[8,16,64]{2,0,1:T(8,128)S(1)} all-gather(f32[8,4,64]{2,0,1:T(8,128)S(1)} %convolution_bitcast_fusion.6), channel_id=1, replica_groups=mesh['leaf'=64,'rhs'=4] {'rhs'}, dimensions={1}, use_global_device_ids=true | all-gather | bytes 40960 | tf_op jit(solution)/shard_map/all_gather | solution.py:151
  347.2 48.4 %all-gather.6 = f32[64,64,8]{1,2,0:T(8,128)S(1)} all-gather(f32[1,64,8]{1,2,0:T(8,128)S(1)} %convolution_bitcast_fusion.15), channel_id=4, replica_groups=mesh['leaf'=64,'rhs'=4] {'leaf'}, dimensions={0}, use_global_device_ids=true | all-gather | bytes 133120 | tf_op jit(solution)/shard_map/all_gather | solution.py:84
  396.3 1.7 reshape.347
  398.1 1.7 reshape.318
  399.8 2.9 bitcast_reduce_fusion
  403.0 47.4 %all_gather.29 = f32[8,128,64]{2,0,1:T(8,128)S(1)} all-gather(f32[8,2,64]{2,0,1:T(8,128)S(1)} %copy-done.37), channel_id=1, replica_groups=mesh['leaf'=64,'rhs'=4] {'leaf'}, dimensions={1}, use_global_device_ids=true | all-gather | bytes 266240 | tf_op jit(solution)/shard_map/all_gather | solution.py:85
  450.4 1.9 collective-permute-start.4
  452.3 4.9 collective-permute-start.5
  457.3 4.3 collective-permute-start.6
  461.6 2.1 collective-permute-start.7
  469.7 1.6 gather_fusion.13
  472.3 48.5 %all-gather.7 = f32[64,64,8]{1,2,0:T(8,128)S(1)} all-gather(f32[1,64,8]{1,2,0:T(8,128)S(1)} %convolution_bitcast_fusion.12), channel_id=5, replica_groups=mesh['leaf'=64,'rhs'=4] {'leaf'}, dimensions={0}, use_global_device_ids=true | all-gather | bytes 133120 | tf_op jit(solution)/shard_map/all_gather | solution.py:103
  526.4 3.5 fusion.7
  530.5 1.6 convolution_bitcast_fusion.8
  532.8 2.2 convolution_bitcast_fusion.2
  538.7 9.3 %convolution_bitcast_fusion = f32[8,32,256]{2,0,1:T(8,128)S(1)} fusion(f32[32,256,256]{2,1,0:T(8,128)} %param.26, f32[32,8,256]{2,1,0:T(8,128)S(1)} %gather_fusion.7, pred[32]{0:T(512)(128)(4,1)S(1)} %copy-done.56), kind=kOutput, calls=%fused_computation.18 | convolution fusion | flops 201392128 | bytes 8912928 | tf_op jit(solution)/shard_map/pij,rpj->rpi/dot_general | solution.py:42
  (273 shorter events, 75.5 us)
Async XLA Ops:
  0.6 80.8 %copy-start = (f32[4,64,256]{2,1,0:T(8,128)S(1)}, f32[4,64,256]{2,1,0:T(8,128)}, u32[]{:S(2)}) copy-start(f32[4,64,256]{2,1,0:T(8,128)} %param.28) | copy-start | bytes 786436
  2.1 77.9 %all-to-all-start = ((f32[2,16,256]{2,0,1:T(2,128)}), f32[2,16,256]{2,0,1:T(2,128)}, u32[]{:S(2)}, u32[]{:S(2)}) async-start(f32[2,16,256]{2,0,1:T(2,128)} %copy.124), calls=%async_computation | async-start | bytes 65536 | tf_op jit(solution)/shard_map/all_to_all | solution.py:184
  28.5 5.5 %copy-start.63 = (s32[1,4]{1,0:T(1,128)S(1)}, s32[1,4]{1,0:T(1,128)}, u32[]{:S(2)}) copy-start(s32[1,4]{1,0:T(1,128)} %param.37) | copy-start | bytes 52
  28.5 7.9 %copy-start.1 = (f32[126,64,64]{0,2,1:T(8,128)S(1)}, f32[126,64,64]{0,2,1:T(8,128)}, u32[]{:S(2)}) copy-start(f32[126,64,64]{0,2,1:T(8,128)} %param.35) | copy-start | bytes 6193156
  67.5 6.0 %copy-start.6 = (f32[1,64,64]{0,2,1:T(8,128)S(1)}, f32[1,64,64]{0,2,1:T(8,128)}, u32[]{:S(2)}) copy-start(f32[1,64,64]{0,2,1:T(8,128)} %get-tuple-element.20) | copy-start | bytes 49156
  70.6 21.6 %copy-start.3 = (f32[28,64,64]{2,1,0:T(8,128)S(1)}, f32[28,64,64]{2,1,0:T(8,128)}, u32[]{:S(2)}) copy-start(f32[28,64,64]{2,1,0:T(8,128)} %param.29) | copy-start | bytes 1376260
  81.4 133.6 %copy-start.2 = (f32[64,64,64]{2,1,0:T(8,128)S(1)}, f32[64,64,64]{2,1,0:T(8,128)}, u32[]{:S(2)}) copy-start(f32[64,64,64]{2,1,0:T(8,128)} %copy.175) | copy-start | bytes 3145732
  92.2 72.5 %copy-start.16 = (f32[8,16,64]{2,0,1:T(8,128)}, f32[8,16,64]{2,0,1:T(8,128)S(1)}, u32[]{:S(2)}) copy-start(f32[8,16,64]{2,0,1:T(8,128)S(1)} %all_gather.24) | copy-start | bytes 98308
  92.7 72.0 %copy-start.25 = (f32[8,8,64]{2,0,1:T(8,128)}, f32[8,8,64]{2,0,1:T(8,128)S(1)}, u32[]{:S(2)}) copy-start(f32[8,8,64]{2,0,1:T(8,128)S(1)} %bitcast_reduce_fusion.7) | copy-start | bytes 49156
  95.1 222.6 %collective-permute-start = (f32[8,4,256]{2,0,1:T(8,128)}, f32[8,4,256]{2,0,1:T(8,128)}, u32[]{:S(2)}, u32[]{:S(2)}) collective-permute-start(f32[8,4,256]{2,0,1:T(8,128)} %all_to_all.16), channel_id=1, source_target_pairs={{0,1},{1,2},{2,3},{3,4},{4,5},{5,6},{6,7},{7,8},{8,9},{9,10},{10,1... | collective-permute-start | bytes 98312 | tf_op jit(solution)/shard_map/ppermute | solution.py:19
  98.2 219.5 %collective-permute-start.1 = (f32[8,4,256]{2,0,1:T(8,128)}, f32[8,4,256]{2,0,1:T(8,128)}, u32[]{:S(2)}, u32[]{:S(2)}) collective-permute-start(f32[8,4,256]{2,0,1:T(8,128)} %all_to_all.16), channel_id=1, source_target_pairs={{1,0},{2,1},{3,2},{4,3},{5,4},{6,5},{7,6},{8,7},{9,8},{10,9},{11,1... | collective-permute-start | bytes 98312 | tf_op jit(solution)/shard_map/ppermute | solution.py:20
  213.1 4.8 copy-start.4
  213.1 5.8 %copy-start.8 = (f32[16,64,64]{2,1,0:T(8,128)S(1)}, f32[16,64,64]{2,1,0:T(8,128)}, u32[]{:S(2)}) copy-start(f32[16,64,64]{2,1,0:T(8,128)} %copy.177) | copy-start | bytes 786436
  215.1 4.9 copy-start.20
  215.1 4.9 copy-start.61
  272.8 19.5 %collective-permute-start.2 = (f32[8,3,3,64]{3,0,2,1:T(8,128)}, f32[8,3,3,64]{3,0,2,1:T(8,128)}, u32[]{:S(2)}, u32[]{:S(2)}) collective-permute-start(f32[8,3,3,64]{3,0,2,1:T(8,128)} %get-tuple-element.38), channel_id=1, source_target_pairs={{0,4},{4,8},{8,12},{12,16},{16,20},{20,24},{24,28},{28,32},{32,36}... | collective-permute-start | bytes 55304 | tf_op jit(solution)/shard_map/ppermute | solution.py:19
  275.3 18.3 %collective-permute-start.3 = (f32[8,3,3,64]{3,0,2,1:T(8,128)}, f32[8,3,3,64]{3,0,2,1:T(8,128)}, u32[]{:S(2)}, u32[]{:S(2)}) collective-permute-start(f32[8,3,3,64]{3,0,2,1:T(8,128)} %get-tuple-element.39), channel_id=1, source_target_pairs={{4,0},{8,4},{12,8},{16,12},{20,16},{24,20},{28,24},{32,28},{36,32}... | collective-permute-start | bytes 55304 | tf_op jit(solution)/shard_map/ppermute | solution.py:20
  297.6 15.0 %copy-start.34 = (f32[16,4]{1,0:T(8,128)S(1)}, f32[16,4]{1,0:T(8,128)}, u32[]{:S(2)}) copy-start(f32[16,4]{1,0:T(8,128)} %copy.129) | copy-start | bytes 772
  297.6 15.0 %copy-start.51 = (pred[16,4]{1,0:T(8,128)(4,1)S(1)}, pred[16,4]{1,0:T(8,128)(4,1)}, u32[]{:S(2)}) copy-start(pred[16,4]{1,0:T(8,128)(4,1)} %copy.127) | copy-start | bytes 196
  304.5 5.2 copy-start.17
  304.5 5.2 copy-start.38
  304.5 5.2 copy-start.39
  309.6 11.8 %copy-start.55 = (pred[32]{0:T(512)(128)(4,1)S(1)}, pred[32]{0:T(512)(128)(4,1)}, u32[]{:S(2)}) copy-start(pred[32]{0:T(512)(128)(4,1)} %get-tuple-element.18) | copy-start | bytes 100
  312.6 5.2 copy-start.31
  321.5 10.5 %copy-start.32 = (f32[4,8,256]{2,1,0:T(8,128)S(1)}, f32[4,8,256]{2,1,0:T(8,128)}, u32[]{:S(2)}) copy-start(f32[4,8,256]{2,1,0:T(8,128)} %fusion.106) | copy-start | bytes 98308
  321.5 10.5 %copy-start.58 = (s32[32]{0:T(128)S(1)}, s32[32]{0:T(128)}, u32[]{:S(2)}) copy-start(s32[32]{0:T(128)} %subtract_bitcast_fusion) | copy-start | bytes 388
  321.5 25.5 %copy-start.14 = (f32[2,64,64]{2,1,0:T(8,128)S(1)}, f32[2,64,64]{2,1,0:T(8,128)}, u32[]{:S(2)}) copy-start(f32[2,64,64]{2,1,0:T(8,128)} %param.32) | copy-start | bytes 98308
  399.8 57.4 %copy-start.44 = (f32[8,3,64]{2,0,1:T(8,128)S(1)}, f32[8,3,64]{2,0,1:T(8,128)}, u32[]{:S(2)}) copy-start(f32[8,3,64]{2,0,1:T(8,128)} %get-tuple-element.60) | copy-start | bytes 18436
  399.8 57.4 %copy-start.45 = (f32[8,3,64]{2,0,1:T(8,128)S(1)}, f32[8,3,64]{2,0,1:T(8,128)}, u32[]{:S(2)}) copy-start(f32[8,3,64]{2,0,1:T(8,128)} %get-tuple-element.61) | copy-start | bytes 18436
  399.8 57.4 %copy-start.42 = (f32[8,3,64]{2,0,1:T(8,128)S(1)}, f32[8,3,64]{2,0,1:T(8,128)}, u32[]{:S(2)}) copy-start(f32[8,3,64]{2,0,1:T(8,128)} %get-tuple-element.56) | copy-start | bytes 18436
  399.8 57.4 %copy-start.43 = (f32[8,3,64]{2,0,1:T(8,128)S(1)}, f32[8,3,64]{2,0,1:T(8,128)}, u32[]{:S(2)}) copy-start(f32[8,3,64]{2,0,1:T(8,128)} %get-tuple-element.57) | copy-start | bytes 18436
  399.8 57.5 %copy-start.40 = (f32[8,3,64]{2,0,1:T(8,128)S(1)}, f32[8,3,64]{2,0,1:T(8,128)}, u32[]{:S(2)}) copy-start(f32[8,3,64]{2,0,1:T(8,128)} %get-tuple-element.40) | copy-start | bytes 18436
  399.8 57.5 %copy-start.41 = (f32[8,3,64]{2,0,1:T(8,128)S(1)}, f32[8,3,64]{2,0,1:T(8,128)}, u32[]{:S(2)}) copy-start(f32[8,3,64]{2,0,1:T(8,128)} %get-tuple-element.41) | copy-start | bytes 18436
  399.8 63.9 %copy-start.5 = (f32[32,64,64]{2,1,0:T(8,128)S(1)}, f32[32,64,64]{2,1,0:T(8,128)}, u32[]{:S(2)}) copy-start(f32[32,64,64]{2,1,0:T(8,128)} %copy.176) | copy-start | bytes 1572868
  399.8 64.8 %copy-start.9 = (f32[16,64,64]{2,1,0:T(8,128)S(1)}, f32[16,64,64]{2,1,0:T(8,128)}, u32[]{:S(2)}) copy-start(f32[16,64,64]{2,1,0:T(8,128)} %copy.177) | copy-start | bytes 786436
  402.8 62.8 %copy-start.13 = (f32[4,64,64]{2,1,0:T(8,128)S(1)}, f32[4,64,64]{2,1,0:T(8,128)}, u32[]{:S(2)}) copy-start(f32[4,64,64]{2,1,0:T(8,128)} %copy.179) | copy-start | bytes 196612
  402.8 63.0 %copy-start.21 = (f32[2,64,64]{2,1,0:T(8,128)S(1)}, f32[2,64,64]{2,1,0:T(8,128)}, u32[]{:S(2)}) copy-start(f32[2,64,64]{2,1,0:T(8,128)} %copy.180) | copy-start | bytes 98308
  403.0 68.4 %copy-start.22 = (f32[1,4,64,64]{3,2,1,0:T(8,128)S(1)}, f32[1,4,64,64]{3,2,1,0:T(8,128)}, u32[]{:S(2)}) copy-start(f32[1,4,64,64]{3,2,1,0:T(8,128)} %param.36) | copy-start | bytes 196612
  450.4 86.7 %collective-permute-start.4 = (f32[8,4,256]{2,1,0:T(4,128)}, f32[8,4,256]{2,1,0:T(4,128)}, u32[]{:S(2)}, u32[]{:S(2)}) collective-permute-start(f32[8,4,256]{2,1,0:T(4,128)} %fusion.13), channel_id=1, source_target_pairs={{0,1},{1,2},{2,3},{3,4},{4,5},{5,6},{6,7},{7,8},{8,9},{9,10},{10,1... | collective-permute-start | bytes 98312 | tf_op jit(solution)/shard_map/ppermute | solution.py:19
  452.3 84.8 %collective-permute-start.5 = (f32[8,4,256]{2,1,0:T(4,128)}, f32[8,4,256]{2,1,0:T(4,128)}, u32[]{:S(2)}, u32[]{:S(2)}) collective-permute-start(f32[8,4,256]{2,1,0:T(4,128)} %fusion.13), channel_id=1, source_target_pairs={{1,0},{2,1},{3,2},{4,3},{5,4},{6,5},{7,6},{8,7},{9,8},{10,9},{11,1... | collective-permute-start | bytes 98312 | tf_op jit(solution)/shard_map/ppermute | solution.py:20
  457.3 68.3 %collective-permute-start.6 = (f32[8,3,3,64]{3,0,2,1:T(8,128)S(1)}, f32[8,3,3,64]{3,0,2,1:T(8,128)S(1)}, u32[]{:S(2)}, u32[]{:S(2)}) collective-permute-start(f32[8,3,3,64]{3,0,2,1:T(8,128)S(1)} %get-tuple-element.36), channel_id=1, source_target_pairs={{0,4},{4,8},{8,12},{12,16},{16,20},{20,24},{24,28},{28,32},{32,36}... | collective-permute-start | bytes 55304 | tf_op jit(solution)/shard_map/ppermute | solution.py:19
  461.6 60.1 %copy-start.11 = (f32[3,4,64,64]{3,2,1,0:T(8,128)S(1)}, f32[3,4,64,64]{3,2,1,0:T(8,128)}, u32[]{:S(2)}) copy-start(f32[3,4,64,64]{3,2,1,0:T(8,128)} %param.33) | copy-start | bytes 589828
  461.6 64.1 %collective-permute-start.7 = (f32[8,3,3,64]{3,0,2,1:T(8,128)S(1)}, f32[8,3,3,64]{3,0,2,1:T(8,128)S(1)}, u32[]{:S(2)}, u32[]{:S(2)}) collective-permute-start(f32[8,3,3,64]{3,0,2,1:T(8,128)S(1)} %get-tuple-element.37), channel_id=1, source_target_pairs={{4,0},{8,4},{12,8},{16,12},{20,16},{24,20},{28,24},{32,28},{36,32}... | collective-permute-start | bytes 55304 | tf_op jit(solution)/shard_map/ppermute | solution.py:20
  464.7 58.8 %copy-start.54 = (f32[2,4]{1,0:T(2,128)S(1)}, f32[2,4]{1,0:T(2,128)}, u32[]{:S(2)}) copy-start(f32[2,4]{1,0:T(2,128)} %get-tuple-element.67) | copy-start | bytes 100
  464.7 59.8 %copy-start.30 = (f32[1,64,64]{2,1,0:T(8,128)S(1)}, f32[1,64,64]{2,1,0:T(8,128)}, u32[]{:S(2)}) copy-start(f32[1,64,64]{2,1,0:T(8,128)} %copy.182) | copy-start | bytes 49156
  464.7 59.8 %copy-start.48 = (f32[8,64]{1,0:T(8,128)S(1)}, f32[8,64]{1,0:T(8,128)}, u32[]{:S(2)}) copy-start(f32[8,64]{1,0:T(8,128)} %fusion.90) | copy-start | bytes 6148
  464.7 59.9 %copy-start.29 = (f32[1,64,64]{2,1,0:T(8,128)S(1)}, f32[1,64,64]{2,1,0:T(8,128)}, u32[]{:S(2)}) copy-start(f32[1,64,64]{2,1,0:T(8,128)} %copy.183) | copy-start | bytes 49156
  464.7 60.1 %copy-start.28 = (f32[1,64,64]{2,1,0:T(8,128)S(1)}, f32[1,64,64]{2,1,0:T(8,128)}, u32[]{:S(2)}) copy-start(f32[1,64,64]{2,1,0:T(8,128)} %copy.184) | copy-start | bytes 49156
  464.7 60.3 %copy-start.27 = (f32[1,64,64]{2,1,0:T(8,128)S(1)}, f32[1,64,64]{2,1,0:T(8,128)}, u32[]{:S(2)}) copy-start(f32[1,64,64]{2,1,0:T(8,128)} %copy.185) | copy-start | bytes 49156
  464.7 60.4 %copy-start.26 = (f32[1,64,64]{2,1,0:T(8,128)S(1)}, f32[1,64,64]{2,1,0:T(8,128)}, u32[]{:S(2)}) copy-start(f32[1,64,64]{2,1,0:T(8,128)} %copy.186) | copy-start | bytes 49156
  464.7 60.6 %copy-start.15 = (f32[2,64,64]{2,1,0:T(8,128)S(1)}, f32[2,64,64]{2,1,0:T(8,128)}, u32[]{:S(2)}) copy-start(f32[2,64,64]{2,1,0:T(8,128)} %param.32) | copy-start | bytes 98308
  465.3 60.4 %copy-start.19 = (f32[8,16,64]{2,0,1:T(8,128)S(1)}, f32[8,16,64]{2,0,1:T(8,128)}, u32[]{:S(2)}) copy-start(f32[8,16,64]{2,0,1:T(8,128)} %copy-done.18) | copy-start | bytes 98308
  465.3 60.5 %copy-start.33 = (s32[1024]{0:T(1024)S(1)}, s32[1024]{0:T(1024)}, u32[]{:S(2)}) copy-start(s32[1024]{0:T(1024)} %get-tuple-element.74) | copy-start | bytes 12292
  465.8 60.6 %copy-start.35 = (f32[16,4]{1,0:T(8,128)S(1)}, f32[16,4]{1,0:T(8,128)}, u32[]{:S(2)}) copy-start(f32[16,4]{1,0:T(8,128)} %copy.129) | copy-start | bytes 772
  465.8 60.6 %copy-start.52 = (pred[16,4]{1,0:T(8,128)(4,1)S(1)}, pred[16,4]{1,0:T(8,128)(4,1)}, u32[]{:S(2)}) copy-start(pred[16,4]{1,0:T(8,128)(4,1)} %copy.127) | copy-start | bytes 196
  521.8 8.2 %copy-start.53 = (s32[1024]{0:T(1024)S(1)}, s32[1024]{0:T(1024)}, u32[]{:S(2)}) copy-start(s32[1024]{0:T(1024)} %get-tuple-element.72) | copy-start | bytes 12292
  523.4 7.1 %copy-start.49 = (f32[4,4]{1,0:T(4,128)S(1)}, f32[4,4]{1,0:T(4,128)}, u32[]{:S(2)}) copy-start(f32[4,4]{1,0:T(4,128)} %copy.135) | copy-start | bytes 196
  523.4 7.1 %copy-start.60 = (pred[4,4]{1,0:T(4,128)(4,1)S(1)}, pred[4,4]{1,0:T(4,128)(4,1)}, u32[]{:S(2)}) copy-start(pred[4,4]{1,0:T(4,128)(4,1)} %copy.133) | copy-start | bytes 52
  525.4 6.8 %copy-start.24 = (f32[8,8,64]{2,0,1:T(8,128)S(1)}, f32[8,8,64]{2,0,1:T(8,128)}, u32[]{:S(2)}) copy-start(f32[8,8,64]{2,0,1:T(8,128)} %copy-done.23) | copy-start | bytes 49156
  525.7 6.5 %copy-start.46 = (s32[1024]{0:T(1024)S(1)}, s32[1024]{0:T(1024)}, u32[]{:S(2)}) copy-start(s32[1024]{0:T(1024)} %get-tuple-element.73) | copy-start | bytes 12292
  525.8 7.0 %copy-start.47 = (f32[8,4]{1,0:T(8,128)S(1)}, f32[8,4]{1,0:T(8,128)}, u32[]{:S(2)}) copy-start(f32[8,4]{1,0:T(8,128)} %copy.132) | copy-start | bytes 388
  525.8 7.0 %copy-start.57 = (pred[8,4]{1,0:T(8,128)(4,1)S(1)}, pred[8,4]{1,0:T(8,128)(4,1)}, u32[]{:S(2)}) copy-start(pred[8,4]{1,0:T(8,128)(4,1)} %copy.130) | copy-start | bytes 100
  532.2 6.6 %copy-start.56 = (pred[32]{0:T(512)(128)(4,1)S(1)}, pred[32]{0:T(512)(128)(4,1)}, u32[]{:S(2)}) copy-start(pred[32]{0:T(512)(128)(4,1)} %get-tuple-element.18) | copy-start | bytes 100
  538.7 9.3 %copy-start.59 = (s32[32]{0:T(128)S(1)}, s32[32]{0:T(128)}, u32[]{:S(2)}) copy-start(s32[32]{0:T(128)} %subtract_bitcast_fusion) | copy-start | bytes 388
  (9 other events, 25.0 us)
where the time goes:
time: 558 us; the launch traced here: 549 us
  blocking collectives  307 us (55%)
  local copies, waits for them, and re-layouts  114 us (20%)
  matrix products  74.3 us (13%)
  starting transfers between devices  34.3 us (6%)
  other arithmetic  17.7 us (3%)
    all_gather x2, blocking collectives, tree_pass(): lax.all_gather(upper_pair, 'leaf', axis=1, tiled=True)  106 us
    all_gather x2, blocking collectives, tree_pass(): lax.all_gather(subtree_root, 'leaf', axis=1, tiled=True)  91.6 us
    all_gather x2, blocking collectives, tree_pass(): ancestor = lax.all_gather(owned_terms, 'leaf', axis=1, tiled=True)  90.5 us
    unnamed x155, local copies, waits for them, and re-layouts  43 us
    dot_general x12, matrix products, couple_lists(): return jnp.einsum('nkab,cnkb->cna', blocks, picked, precision=highest)  21.4 us
    dot_general x2, matrix products, near_field(): terms = jnp.einsum('pij,rpj->rpi', near_blocks, picked, precision=highest)  19.8 us
    all_gather x2, blocking collectives, apply_matrix(): leaf_coeffs = lax.all_gather(own_coeffs, 'rhs', axis=1, tiled=True)  19.1 us
    gather x12, local copies, waits for them, and re-layouts, couple_lists(): picked = jnp.take(table, clipped, axis=1)  18.1 us
  transfers between devices with their start and end apart: 9, of which 1 were waited for; matrix products, arithmetic and copies ran while one was open for 29% of the time, Pallas kernels for 0%

commit v1 on v0

v1 whole, which is shorter than its diff:
```python
import jax
import jax.numpy as jnp
from jax import lax
from jax.experimental import pallas as pl
from jax.experimental.pallas import tpu as pltpu
from jax.sharding import PartitionSpec as P

F32 = jnp.float32
BF16 = jnp.bfloat16
MESH = pl.DeviceIdType.MESH
NN = (((1,), (0,)), ((), ()))
NT = (((1,), (1,)), ((), ()))
XY = [(i, k) for i in range(4) for k in range(4) if (i, k) != (0, 0)]
XY_ORDER = sorted(XY, key=lambda s: -(min(s[0], 4 - s[0]) + min(s[1], 4 - s[1])))
ZC_ORDER = [(4, 0), (4, 1), (3, 0), (3, 1), (5, 0), (5, 1), (2, 0), (2, 1), (6, 0), (6, 1), (1, 0), (1, 1), (7, 0), (7, 1), (0, 1)]
NEAR_D = (1, -1, 2, -2, 3, -3, 4, -4, 8, -8)


def stacked(x):
    high = x.astype(BF16).astype(F32)
    return jnp.concatenate([high, x - high], axis=0).astype(BF16)


def parts(w):
    high = w.astype(BF16)
    return high, (w - high.astype(F32)).astype(BF16)


def dot(x, w, dims):
    return lax.dot_general(x, w, dims, preferred_element_type=F32)


def mm_parts(xs, high, low, dims):
    y = dot(xs, high, dims) + dot(xs, low, dims)
    rows = xs.shape[0] // 2
    return y[:rows] + y[rows:]


def mm(x, w, dims):
    return mm_parts(stacked(x), *parts(w), dims)


def left_lanes(shape):
    return lax.broadcasted_iota(jnp.int32, shape, len(shape) - 1) < 64


def swap(x):
    return pltpu.roll(x, 64, x.ndim - 1)


def kernel(
    pairs, local_lists, middle_lists, upper_lists,
    columns, near_hbm, basis_hbm, lt_hbm, lc_hbm, mt_hbm, mc_hbm, ut_hbm, uc_hbm,
    first_hbm, second_hbm,
    vin, vlf, vnext, near, basis, e10, e9, e8, e7, k10, k9, k8, k7, k6, ut, uc,
    dsend, dbuf, abuf, ahigh, alow, wup, q6s, q7s, q8s,
    halo_0, halo_1, xybuf, agsend, agbuf, c7_0, c7_1, acc, outs,
    load_sem, in_send, in_recv, edge_send, edge_recv, d_send, d_recv,
    xy_send, xy_recv, halo_send, halo_recv, ag_send, ag_recv, c7_send, c7_recv, v_send, v_recv, out_sem,
):
    halo, c7buf = (halo_0, halo_1), (c7_0, c7_1)
    g = lax.axis_index("leaf")
    q = lax.axis_index("rhs")
    d = 4 * g + q
    gx = g // 16
    zc = lax.rem(g, 16)
    gz, gc = zc // 2, lax.rem(zc, 2)

    def linear(k):
        e = lax.rem(d + k + 256, 256)
        return (e // 4, lax.rem(e, 4))

    def group(k):
        return lax.rem(g + k + 64, 64)

    def xy(i, k):
        return (lax.rem(gx + i, 4) * 16 + zc, lax.rem(q + k, 4))

    def zcs(i, k):
        return (gx * 16 + lax.rem(gz + i, 8) * 2 + lax.rem(gc + k, 2), q)

    loads = []

    def load(src, dst):
        c = pltpu.make_async_copy(src, dst, load_sem.at[len(loads)])
        c.start()
        loads.append(c)
        return c

    ld_own = load(columns, vin.at[pl.ds(2 * q, 2), 8:24])
    ld_uc = load(uc_hbm.at[0], uc)
    ld_basis = load(basis_hbm, basis)
    ld_e = [
        load(lt_hbm.at[pl.ds(12 + 4 * q, 4)], e10),
        load(lt_hbm.at[pl.ds(4 + 2 * q, 2)], e9),
        load(lt_hbm.at[q], e8),
        load(mt_hbm.at[q // 2], e7),
    ]
    ld_near = load(near_hbm, near)
    ld_k = [
        load(lc_hbm.at[pl.ds(12 + 4 * q, 4)], k10),
        load(lc_hbm.at[pl.ds(4 + 2 * q, 2)], k9),
        load(lc_hbm.at[q], k8),
        load(mc_hbm.at[1 + q // 2], k7),
        load(mc_hbm.at[0], k6),
    ]
    ld_ut = load(ut_hbm, ut)

    level = 2 + (g >= 8).astype(jnp.int32) + (g >= 16).astype(jnp.int32) + (g >= 32).astype(jnp.int32)
    count = jnp.where(g >= 32, 2, jnp.where(g >= 16, 4, jnp.where(g >= 8, 8, jnp.where(g >= 4, 16, 0))))
    start = jnp.where(g >= 32, 32, jnp.where(g >= 16, 16, jnp.where(g >= 8, 8, 4)))
    own_number = g - start
    first_below = own_number * count
    own_inside = jnp.where((g >= first_below) & (g < first_below + count), 1, 0)
    barrier = pltpu.get_barrier_semaphore()

    def greet(device):
        pl.semaphore_signal(barrier, inc=1, device_id=device, device_id_type=MESH)

    owners = [2**t + g // 2 ** (6 - t) for t in range(2, 6)]
    for s in XY_ORDER:
        greet(xy(*s))
    for s in ZC_ORDER:
        greet(zcs(*s))
    for k in NEAR_D:
        greet(linear(k))
    for owner in owners:
        @pl.when(owner != g)
        def _():
            greet((owner, q))
    pl.semaphore_wait(barrier, 15 + 15 + len(NEAR_D) + count - own_inside)

    def remote(src, dst, ss, rs, device):
        c = pltpu.make_async_remote_copy(
            src_ref=src, dst_ref=dst, send_sem=ss, recv_sem=rs, device_id=device, device_id_type=MESH
        )
        c.start()
        return c

    sent = []
    ins = []
    for k in (2, 1, 3):
        ins.append(
            remote(columns, vin.at[pl.ds(2 * q, 2), 8:24], in_send.at[k], in_recv.at[k], (g, lax.rem(q + k, 4)))
        )
    sent.append(remote(columns.at[:, 8:16], vin.at[pl.ds(2 * q, 2), 0:8], edge_send.at[0], edge_recv.at[0, q], (group(1), 0)))
    sent.append(remote(columns.at[:, 0:8], vin.at[pl.ds(2 * q, 2), 24:32], edge_send.at[1], edge_recv.at[1, q], (group(-1), 3)))

    def by_offset(blocks, entries, number):
        found = []
        for offset in (-3, -2, 2, 3):
            total = None
            for k in range(4):
                weight = jnp.where((entries[k] >= 0) & (entries[k] == number + offset), 1.0, 0.0)
                term = blocks[k] * weight
                total = term if total is None else total + term
            found.append(total)
        return (jnp.concatenate(found[:2], axis=1), jnp.concatenate(found[2:], axis=1))

    ld_uc.wait()
    low_half, high_half = by_offset(uc, [upper_lists[0, k] for k in range(4)], own_number)
    dsend[0] = low_half
    dsend[1] = high_half

    def give(i, carry):
        to = first_below + i

        @pl.when(to != g)
        def _():
            remote(dsend, dbuf.at[level - 2], d_send.at[i], d_recv.at[level - 2], (to, q))

        @pl.when(to == g)
        def _():
            pltpu.make_async_copy(dsend, dbuf.at[level - 2], d_recv.at[level - 2]).start()

        return carry

    lax.fori_loop(0, count, give, 0)

    for c in ld_e:
        c.wait()
    q8 = jnp.concatenate([mm(e10[l], e9[l // 2], NN) for l in range(4)], axis=0)
    q7 = mm(q8, e8[...], NN)
    q6 = mm(q7, e7[...], NN)
    q8s[...] = q8
    q7s[...] = q7
    q6s[...] = q6
    wup[:, 0:128] = jnp.concatenate([q7, q6], axis=1)
    wup[:, 128:256] = jnp.concatenate([q8, q8], axis=1)

    left = left_lanes((8, 128))
    quarter = lax.broadcasted_iota(jnp.int32, (8, 256), 1) // 64
    ld_own.wait()
    ld_basis.wait()
    for c in ins:
        c.wait_recv()
    sent.extend(ins)
    for i in range(16):
        vlf[4 + i] = vin[:, 8 + i, :]

    def climb(p, rows):
        wide = mm(rows, basis[...].reshape(256, 256), NT)
        c10 = jnp.zeros((8, 256), F32)
        for l in range(4):
            c10 = jnp.where(quarter == l, wide[8 * l : 8 * l + 8], c10)
        tops = mm(c10, wup[...], NN)
        xybuf[p, 0, 0] = tops[:, 0:128]
        halo[p][3, 3] = tops[:, 128:256]
        for i, k in XY_ORDER:
            xys[p].append(
                remote(xybuf.at[p, 0, 0], xybuf.at[p, i, k], xy_send.at[p, i, k], xy_recv.at[p, i, k], xy(i, k))
            )
        halo[p][3, 0] = c10[:, 0:128]
        halo[p][3, 1] = c10[:, 128:256]
        halo[p][3, 2] = jnp.concatenate(
            [mm(c10[:, 128 * j : 128 * j + 128], e10[2 * j : 2 * j + 2].reshape(128, 64), NN) for j in range(2)], axis=1
        )
        for k in (1, -1, 2, -2, 3, -3):
            tiles = pl.ds({1: 0, 2: 2, 3: 3}[abs(k)], {1: 4, 2: 2, 3: 1}[abs(k)])
            halos[p].append(
                remote(
                    halo[p].at[3, tiles], halo[p].at[3 - k, tiles], halo_send.at[p, 3 - k], halo_recv.at[p, 3 - k], linear(k)
                )
            )

    xys, halos, ags, c7s = ([], []), ([], []), ([], []), ([], [])

    def near_field(vectors, offset, least):
        def step(s, totals):
            target = pairs[0, s] - 4 * d
            source = jnp.clip(pairs[1, s] - offset, least, least + 11)
            term = mm(vectors[source], near[s], NT)
            return tuple(t + term * jnp.where(target == l, 1.0, 0.0) for l, t in enumerate(totals))

        zero = jnp.zeros((8, 256), F32)
        totals = lax.fori_loop(0, 32, step, (zero,) * 4, unroll=4)
        for l in range(4):
            acc[8 * l : 8 * l + 8] = totals[l]

    def half_of(tile, half):
        return jnp.where(half == 1, swap(tile), tile)[:, 0:64]

    def coupled(blocks, entries, pick):
        total = None
        for k in range(4):
            x = pick(entries[k]) * jnp.where(entries[k] >= 0, 1.0, 0.0)
            term = mm(x, blocks[k], NT)
            total = term if total is None else total + term
        return total

    def local_coupled(p):
        for c in halos[p]:
            c.wait_recv()
        sent.extend(halos[p])

        def pick10(entry):
            at = jnp.clip(entry - 4 * d + 12, 0, 27)
            return half_of(halo[p][at // 4, lax.rem(at, 4) // 2], lax.rem(at, 2))

        def pick9(entry):
            at = jnp.clip(entry - 2 * d + 6, 0, 13)
            return half_of(halo[p][at // 2, 2], lax.rem(at, 2))

        def pick8(entry):
            at = jnp.clip(entry - d + 3, 0, 6)
            return halo[p][at, 3][:, 0:64]

        z10 = [coupled(k10[l], [local_lists[k, 12 + 4 * q + l] for k in range(4)], pick10) for l in range(4)]
        z9 = [coupled(k9[j], [local_lists[k, 4 + 2 * q + j] for k in range(4)], pick9) for j in range(2)]
        z8 = coupled(k8, [local_lists[k, q] for k in range(4)], pick8)
        down = mm(z8, q8s[...], NT)
        below = [mm(z9[j], e10[2 * j : 2 * j + 2].reshape(128, 64), NT) for j in range(2)]
        return down + jnp.concatenate(
            [below[0] + jnp.concatenate(z10[0:2], axis=1), below[1] + jnp.concatenate(z10[2:4], axis=1)], axis=1
        )

    def middle(p):
        for c in xys[p]:
            c.wait_recv()
        sent.extend(xys[p])
        totals = []
        for x in range(4):
            i = lax.rem(gx - x + 4, 4)
            totals.append(xybuf[p, i, 0] + xybuf[p, i, 1] + xybuf[p, i, 2] + xybuf[p, i, 3])
        for j in range(2):
            agsend[p, j] = jnp.where(left, swap(totals[2 * j]), totals[2 * j + 1])
        for i, k in ZC_ORDER:
            ags[p].append(
                remote(agsend.at[p], agbuf.at[p, i, k], ag_send.at[p, i, k], ag_recv.at[p, i, k], zcs(i, k))
            )
        agbuf[p, 0, 0] = agsend[p]

        def own(y):
            return xybuf[p, 0, lax.rem(q - y + 4, 4)]

        c7buf[p][2] = jnp.where(left, own(0) + own(1), swap(own(2) + own(3)))
        for k in (1, -1, 2, -2):
            c7s[p].append(
                remote(c7buf[p].at[2], c7buf[p].at[2 - k], c7_send.at[p, 2 - k], c7_recv.at[p, 2 - k], (group(k), q))
            )

    def middle_coupled(p):
        for c in c7s[p]:
            c.wait_recv()
        sent.extend(c7s[p])

        def pick7(entry):
            at = jnp.clip(entry - 2 * g + 4, 0, 9)
            return half_of(c7buf[p][at // 2], lax.rem(at, 2))

        z7 = coupled(k7, [middle_lists[1 + q // 2, k] for k in range(4)], pick7)
        return mm(z7, q7s[...], NT)

    def upper_operator():
        offsets = {2: 0, 3: 2, 4: 6, 5: 14, 6: 30}
        lefts = left_lanes((64, 128))
        ld_ut.wait()

        def transfer(t):
            return ut[2**t - 2 + g // 2 ** (6 - t)]

        chain = {5: transfer(6)}
        for t in (4, 3, 2, 1, 0):
            chain[t] = mm(chain[t + 1], transfer(t + 1), NN)
        ld_k[4].wait()

        def add(t, lower, upper):
            number = g // 2 ** (6 - t)
            for j, offset in enumerate((-3, -2, 2, 3)):
                at = jnp.clip(number + offset, 0, 2**t - 1)
                block = lower if offset < 0 else upper
                block = jnp.where(lax.rem(at, 2) == j % 2, block, swap(block))
                kept = jnp.where(lefts == (lax.rem(at, 2) == 0), block, 0.0)
                abuf[offsets[t] + at // 2] = abuf[offsets[t] + at // 2] + kept

        abuf[0:2] = jnp.zeros((2, 64, 128), F32)
        for t in range(2, 6):
            pltpu.make_async_copy(dbuf.at[t - 2], dbuf.at[t - 2], d_recv.at[t - 2]).wait()
            add(t, mm(chain[t], dbuf[t - 2, 0], NN), mm(chain[t], dbuf[t - 2, 1], NN))

            def widen(i, carry):
                tile = abuf[offsets[t] + i]
                for half in range(2):
                    x = tile[:, 0:64] if half == 0 else swap(tile)[:, 0:64]
                    n = 2 * i + half
                    e = ut[pl.ds(2 ** (t + 1) - 2 + 2 * n, 2)].reshape(128, 64)
                    abuf[offsets[t + 1] + n] = mm(x, e, NT)
                return carry

            lax.fori_loop(0, 2 ** (t - 1), widen, 0, unroll=2)
        add(6, *by_offset(k6, [middle_lists[0, k] for k in range(4)], g))

        def keep(i, carry):
            high, low = parts(abuf[30 + i])
            ahigh[i] = high
            alow[i] = low
            return carry

        lax.fori_loop(0, 32, keep, 0, unroll=4)
        root = jnp.zeros((8, 64), F32)
        return mm(root, chain[0], NT)

    def upper(p):
        for c in ags[p]:
            c.wait_recv()
        sent.extend(ags[p])
        total = None
        for x in range(2):
            for z in range(8):
                zslot = lax.rem(gz - z + 8, 8)
                even = agbuf[p, zslot, gc, x]
                odd = agbuf[p, zslot, 1 - gc, x]
                for h in range(2):
                    both = jnp.where(left, even, swap(odd)) if h == 0 else jnp.where(left, swap(even), odd)
                    i = (2 * x + h) * 8 + z
                    xs = stacked(both)
                    term = dot(xs, ahigh[i], NT) + dot(xs, alow[i], NT)
                    total = term if total is None else total + term
        return total[:8] + total[8:]

    def finish(p, base, w6):
        w10 = base + mm(w6, q6s[...], NT)
        spread = jnp.concatenate([jnp.where(quarter == l, w10, 0.0) for l in range(4)], axis=0)
        rows = mm(spread, basis[...].reshape(256, 256), NN) + acc[...]
        for l in range(4):
            outs[p, l] = rows[8 * l : 8 * l + 8]
        return rows

    rows = jnp.concatenate([vlf[4 + 4 * q + l] for l in range(4)], axis=0)
    climb(0, rows)

    @pl.when(q == 0)
    def _():
        for k in range(4):
            view = vin.at[2 * k : 2 * k + 2, 0:8]
            pltpu.make_async_copy(view, view, edge_recv.at[0, k]).wait()
        for i in range(4):
            vlf[i] = vin[:, 4 + i, :]

    @pl.when(q == 3)
    def _():
        for k in range(4):
            view = vin.at[2 * k : 2 * k + 2, 24:32]
            pltpu.make_async_copy(view, view, edge_recv.at[1, k]).wait()
        for i in range(4):
            vlf[20 + i] = vin[:, 24 + i, :]

    ld_near.wait()
    near_field(vlf, 16 * g - 4, 4 * q)
    middle(0)
    for c in ld_k[:4]:
        c.wait()
    root_part = upper_operator()
    base = local_coupled(0) + middle_coupled(0)
    first = finish(0, base, upper(0) + root_part)
    for l in range(4):
        vnext[4 + l] = first[8 * l : 8 * l + 8]
    vs = [
        remote(vnext.at[4:8], vnext.at[0:4], v_send.at[0], v_recv.at[0], linear(1)),
        remote(vnext.at[4:8], vnext.at[8:12], v_send.at[1], v_recv.at[1], linear(-1)),
    ]
    out0 = pltpu.make_async_copy(outs.at[0], first_hbm, out_sem.at[0])
    out0.start()

    climb(1, first)
    for c in vs:
        c.wait_recv()
    sent.extend(vs)
    near_field(vnext, 4 * d - 4, 0)
    middle(1)
    base = local_coupled(1) + middle_coupled(1)
    finish(1, base, upper(1) + root_part)
    out1 = pltpu.make_async_copy(outs.at[1], second_hbm, out_sem.at[1])
    out1.start()

    for c in sent:
        c.wait_send()

    def given(i, carry):
        @pl.when(first_below + i != g)
        def _():
            pltpu.make_async_copy(dsend, dsend, d_send.at[i]).wait()

        return carry

    lax.fori_loop(0, count, given, 0)
    out0.wait()
    out1.wait()


def body(
    input_columns,
    near_blocks,
    near_pairs,
    leaf_basis,
    local_transfer,
    local_coupling,
    local_lists,
    middle_transfer,
    middle_coupling,
    middle_lists,
    upper_transfer,
    upper_coupling,
    upper_lists,
):
    smem = pl.BlockSpec(memory_space=pltpu.SMEM)
    anywhere = pl.BlockSpec(memory_space=pl.ANY)
    vm = lambda *shape: pltpu.VMEM(shape, F32)
    dma = lambda *shape: pltpu.SemaphoreType.DMA(shape)
    first, second = pl.pallas_call(
        kernel,
        out_shape=[jax.ShapeDtypeStruct((4, 8, 256), F32)] * 2,
        in_specs=[smem] * 4 + [anywhere] * 9,
        out_specs=[anywhere] * 2,
        scratch_shapes=[
            vm(8, 32, 256), vm(24, 8, 256), vm(12, 8, 256), vm(32, 256, 256), vm(4, 64, 256),
            vm(4, 64, 64), vm(2, 64, 64), vm(64, 64), vm(64, 64),
            vm(4, 4, 64, 64), vm(2, 4, 64, 64), vm(4, 64, 64), vm(4, 64, 64), vm(4, 64, 64),
            vm(126, 64, 64), vm(4, 64, 64),
            vm(2, 64, 128), vm(4, 2, 64, 128), vm(62, 64, 128),
            pltpu.VMEM((32, 64, 128), BF16), pltpu.VMEM((32, 64, 128), BF16),
            vm(256, 256), vm(256, 64), vm(256, 64), vm(256, 64),
            vm(7, 4, 8, 128), vm(7, 4, 8, 128), vm(2, 4, 4, 8, 128), vm(2, 2, 8, 128), vm(2, 8, 2, 2, 8, 128),
            vm(5, 8, 128), vm(5, 8, 128), vm(32, 256), vm(2, 4, 8, 256),
            dma(16), dma(4), dma(4), dma(2), dma(2, 4), dma(16), dma(4),
            dma(2, 4, 4), dma(2, 4, 4), dma(2, 7), dma(2, 7), dma(2, 8, 2), dma(2, 8, 2),
            dma(2, 5), dma(2, 5), dma(2), dma(2), dma(2),
        ],
        compiler_params=pltpu.CompilerParams(
            collective_id=0, has_side_effects=True, vmem_limit_bytes=48 * 2**20
        ),
    )(
        near_pairs.T, local_lists.T, middle_lists, upper_lists,
        input_columns, near_blocks, leaf_basis, local_transfer, local_coupling,
        middle_transfer, middle_coupling, upper_transfer, upper_coupling,
    )
    return (first.transpose(1, 0, 2), second.transpose(1, 0, 2))


def solution(mesh):
    in_specs = (
        P("rhs", "leaf", None),
        P(("leaf", "rhs"), None, None),
        P(("leaf", "rhs"), None),
        P(("leaf", "rhs"), None, None),
        P("leaf", None, None),
        P("leaf", None, None, None),
        P("leaf", None),
        P("leaf", None, None),
        P("leaf", None, None, None),
        P("leaf", None),
        P(),
        P("leaf", None, None, None),
        P("leaf", None),
    )
    out_specs = (P(None, ("leaf", "rhs"), None), P(None, ("leaf", "rhs"), None))
    return jax.shard_map(body, mesh=mesh, in_specs=in_specs, out_specs=out_specs, check_vma=False)
```

time: 558 us -> 73.8 us (0.13); the launches traced: 549 us -> 73.7 us
  blocking collectives: 307 us -> 0 us
  local copies, waits for them, and re-layouts: 114 us -> 9.02 us
  matrix products: 74.3 us -> 0 us
  Pallas kernels: 0 us -> 63.9 us
  starting transfers between devices: 34.3 us -> 0 us
  other arithmetic: 17.7 us -> 0 us
    all_gather x8 -> x0, blocking collectives: 307 us -> none  [the longest x2 106 us: tree_pass(): lax.all_gather(upper_pair, 'leaf', axis=1, tiled=True)]
    dot_general x59 -> x0, matrix products: 74.3 us -> none  [the longest x12 21.4 us: couple_lists(): return jnp.einsum('nkab,cnkb->cna', blocks, picked, precision=highest)]
    pallas_call x0 -> x1, Pallas kernels: none -> 63.9 us  [body(): pl.pallas_call(kernel, out_shape=[jax.ShapeDtypeStruct((4, 8, 256), F32)]...]
    unnamed x155 -> x25, local copies, waits for them, and re-layouts: 43 us -> 9.02 us
    ppermute x8 -> x0, starting transfers between devices: 29.3 us -> none  [the longest x4 17.4 us: with_halo(): after = lax.ppermute(leading, axis, down)]
    gather x14 -> x0, local copies, waits for them, and re-layouts: 21.1 us -> none  [the longest x12 18.1 us: couple_lists(): picked = jnp.take(table, clipped, axis=1)]
    dynamic_slice x3 -> x0, local copies, waits for them, and re-layouts: 14 us -> none  [the longest x1 13.1 us: tree_pass(): lax.dynamic_index_in_dim(upper_transfer, groups - 2 + group, 0, keepdims=...]
    slice x13 -> x0, local copies, waits for them, and re-layouts: 14 us -> none  [the longest x5 9.67 us: tree_pass(): upper_transfer[lower_end - 2:2 * lower_end - 2]]
  transfers between devices with their start and end apart: 9 -> 0, of which waited for: 1 -> 0; matrix products, arithmetic and copies ran while one was open for 29% -> 0% of each run, Pallas kernels for 0% -> 0%
where the time goes in v1:
time: 73.8 us; the launch traced here: 73.7 us
  Pallas kernels  63.9 us (87%)
  local copies, waits for them, and re-layouts  9.02 us (12%)
  between operations  0.79 us (1%)
    pallas_call x1, Pallas kernels, body(): pl.pallas_call(kernel, out_shape=[jax.ShapeDtypeStruct((4, 8, 256), F32)]...  63.9 us
    unnamed x25, local copies, waits for them, and re-layouts  9.02 us

profile of v1, /device:TPU:1, one launch (start us, length us, event | category | flops | bytes accessed | tf_op | source)
XLA Modules:
  0.0 73.7 jit_solution(10869524879524699633)
XLA Ops:
  0.6 0.0 copy-start.10
  0.6 0.0 copy-start.4
  0.7 0.0 copy-start.8
  0.7 0.0 copy-start.2
  0.7 0.0 copy-start.5
  0.7 0.0 copy-start.7
  0.7 0.0 copy-start.1
  0.7 0.0 copy-start.3
  0.7 0.0 copy-start.9
  0.7 0.0 copy-start.6
  0.7 5.7 %copy.15.ut_hbm = f32[126,64,64]{2,1,0:T(8,128)} copy(f32[126,64,64]{0,2,1:T(8,128)} %param.23) | data formatting | bytes 4128768 | tf_op args[10]
  6.4 0.0 copy-done.10
  6.4 0.0 copy-done.4
  6.4 0.0 copy-done.8
  6.4 0.0 copy-done.2
  6.4 0.0 copy-done.5
  6.5 0.0 copy-done.7
  6.5 0.0 copy-done.1
  6.5 0.0 copy-done.3
  6.5 0.0 copy-done.9
  6.5 0.0 copy-done.6
  6.5 0.0 copy-start
  6.5 2.0 %copy-done = f32[28,4,64,64]{3,2,1,0:T(8,128)S(1)} copy-done((f32[28,4,64,64]{3,2,1,0:T(8,128)S(1)}, f32[28,4,64,64]{3,2,1,0:T(8,128)}, u32[]{:S(2)}) %copy-start) | copy-done | bytes 1835032
  8.5 63.9 %shard_map.140 = (f32[4,8,256]{2,1,0:T(8,128)S(1)}, f32[4,8,256]{2,1,0:T(8,128)S(1)}) custom-call(s32[2,32]{1,0:T(2,128)S(1)} %bitcast.7, s32[4,28]{1,0:T(4,128)S(1)} %bitcast.6, s32[3,4]{1,0:T(4,128)S(1)} %copy-done.8, s32[1,4]{1,0:T(1,128)S(1)} %copy-done.10, f32[2,16,256]{2,1,0:T(8,128)S(1)} %copy-done.6, f32[32,256,256]{2,1,0:T(8,128)} %near_hbm.1, ...), custom_call_target="tpu_custom_call" | custom-call | tf_op jit(solution)/shard_map/pallas_call | solution.py:470
  72.4 0.6 copy.16
  73.1 0.6 copy.17
Async XLA Ops:
  0.6 5.8 %copy-start.10 = (s32[1,4]{1,0:T(1,128)S(1)}, s32[1,4]{1,0:T(1,128)}, u32[]{:S(2)}) copy-start(s32[1,4]{1,0:T(1,128)} %upper_lists.1) | copy-start | bytes 52
  0.6 5.8 %copy-start.4 = (f32[1,4,64,64]{3,2,1,0:T(8,128)S(1)}, f32[1,4,64,64]{3,2,1,0:T(8,128)}, u32[]{:S(2)}) copy-start(f32[1,4,64,64]{3,2,1,0:T(8,128)} %uc_hbm.1) | copy-start | bytes 196612
  0.7 5.8 %copy-start.8 = (s32[3,4]{1,0:T(4,128)S(1)}, s32[3,4]{1,0:T(4,128)}, u32[]{:S(2)}) copy-start(s32[3,4]{1,0:T(4,128)} %middle_lists.1) | copy-start | bytes 148
  0.7 5.8 %copy-start.2 = (f32[3,4,64,64]{3,2,1,0:T(8,128)S(1)}, f32[3,4,64,64]{3,2,1,0:T(8,128)}, u32[]{:S(2)}) copy-start(f32[3,4,64,64]{3,2,1,0:T(8,128)} %mc_hbm.1) | copy-start | bytes 589828
  0.7 5.8 %copy-start.5 = (f32[2,64,64]{2,1,0:T(8,128)S(1)}, f32[2,64,64]{2,1,0:T(8,128)}, u32[]{:S(2)}) copy-start(f32[2,64,64]{2,1,0:T(8,128)} %mt_hbm.1) | copy-start | bytes 98308
  0.7 5.8 %copy-start.7 = (s32[28,4]{0,1:T(4,128)S(1)}, s32[28,4]{0,1:T(4,128)}, u32[]{:S(2)}) copy-start(s32[28,4]{0,1:T(4,128)} %param.19) | copy-start | bytes 1348
  0.7 5.8 %copy-start.1 = (f32[28,64,64]{2,1,0:T(8,128)S(1)}, f32[28,64,64]{2,1,0:T(8,128)}, u32[]{:S(2)}) copy-start(f32[28,64,64]{2,1,0:T(8,128)} %lt_hbm.1) | copy-start | bytes 1376260
  0.7 5.8 %copy-start.3 = (f32[4,64,256]{2,1,0:T(8,128)S(1)}, f32[4,64,256]{2,1,0:T(8,128)}, u32[]{:S(2)}) copy-start(f32[4,64,256]{2,1,0:T(8,128)} %basis_hbm.1) | copy-start | bytes 786436
  0.7 5.8 %copy-start.9 = (s32[32,2]{0,1:T(2,128)S(1)}, s32[32,2]{0,1:T(2,128)}, u32[]{:S(2)}) copy-start(s32[32,2]{0,1:T(2,128)} %param.15) | copy-start | bytes 772
  0.7 5.8 %copy-start.6 = (f32[2,16,256]{2,1,0:T(8,128)S(1)}, f32[2,16,256]{2,1,0:T(8,128)}, u32[]{:S(2)}) copy-start(f32[2,16,256]{2,1,0:T(8,128)} %columns.1) | copy-start | bytes 98308
  6.5 2.0 %copy-start = (f32[28,4,64,64]{3,2,1,0:T(8,128)S(1)}, f32[28,4,64,64]{3,2,1,0:T(8,128)}, u32[]{:S(2)}) copy-start(f32[28,4,64,64]{3,2,1,0:T(8,128)} %lc_hbm.1) | copy-start | bytes 5505028

commit v2 on v1

--- a/solution.py
+++ b/solution.py
@@ -13,7 +13,7 @@
 XY = [(i, k) for i in range(4) for k in range(4) if (i, k) != (0, 0)]
 XY_ORDER = sorted(XY, key=lambda s: -(min(s[0], 4 - s[0]) + min(s[1], 4 - s[1])))
 ZC_ORDER = [(4, 0), (4, 1), (3, 0), (3, 1), (5, 0), (5, 1), (2, 0), (2, 1), (6, 0), (6, 1), (1, 0), (1, 1), (7, 0), (7, 1), (0, 1)]
-NEAR_D = (1, -1, 2, -2, 3, -3, 4, -4, 8, -8)
+ZC_NEAR = [(2, 0), (2, 1), (6, 0), (6, 1), (1, 0), (1, 1), (7, 0), (7, 1), (0, 1)]
 
 
 def stacked(x):
@@ -52,11 +52,12 @@
     pairs, local_lists, middle_lists, upper_lists,
     columns, near_hbm, basis_hbm, lt_hbm, lc_hbm, mt_hbm, mc_hbm, ut_hbm, uc_hbm,
     first_hbm, second_hbm,
-    vin, vlf, vnext, near, basis, e10, e9, e8, e7, k10, k9, k8, k7, k6, ut, uc,
-    dsend, dbuf, abuf, ahigh, alow, wup, q6s, q7s, q8s,
+    vin, vlf, vnext, near, basis, e10, e9, e8, e7, k10, k9, k8, k7, k6, utt, ut, uc,
+    dsend, dbuf, u_high, u_low, v_high, v_low, gmap, ctile, wup, q6s, q7s, q8s,
     halo_0, halo_1, xybuf, agsend, agbuf, c7_0, c7_1, acc, outs,
     load_sem, in_send, in_recv, edge_send, edge_recv, d_send, d_recv,
     xy_send, xy_recv, halo_send, halo_recv, ag_send, ag_recv, c7_send, c7_recv, v_send, v_recv, out_sem,
+    ready_xy, ready_z, ready_group, ready_plane,
 ):
     halo, c7buf = (halo_0, halo_1), (c7_0, c7_1)
     g = lax.axis_index("leaf")
@@ -88,15 +89,15 @@
         return c
 
     ld_own = load(columns, vin.at[pl.ds(2 * q, 2), 8:24])
-    ld_uc = load(uc_hbm.at[0], uc)
-    ld_basis = load(basis_hbm, basis)
+    ld_ut = load(ut_hbm, utt)
     ld_e = [
         load(lt_hbm.at[pl.ds(12 + 4 * q, 4)], e10),
         load(lt_hbm.at[pl.ds(4 + 2 * q, 2)], e9),
         load(lt_hbm.at[q], e8),
         load(mt_hbm.at[q // 2], e7),
     ]
-    ld_near = load(near_hbm, near)
+    ld_basis = load(basis_hbm, basis)
+    ld_uc = load(uc_hbm.at[0], uc)
     ld_k = [
         load(lc_hbm.at[pl.ds(12 + 4 * q, 4)], k10),
         load(lc_hbm.at[pl.ds(4 + 2 * q, 2)], k9),
@@ -104,7 +105,7 @@
         load(mc_hbm.at[1 + q // 2], k7),
         load(mc_hbm.at[0], k6),
     ]
-    ld_ut = load(ut_hbm, ut)
+    ld_near = load(near_hbm, near)
 
     level = 2 + (g >= 8).astype(jnp.int32) + (g >= 16).astype(jnp.int32) + (g >= 32).astype(jnp.int32)
     count = jnp.where(g >= 32, 2, jnp.where(g >= 16, 4, jnp.where(g >= 8, 8, jnp.where(g >= 4, 16, 0))))
@@ -117,18 +118,20 @@
     def greet(device):
         pl.semaphore_signal(barrier, inc=1, device_id=device, device_id_type=MESH)
 
-    owners = [2**t + g // 2 ** (6 - t) for t in range(2, 6)]
-    for s in XY_ORDER:
-        greet(xy(*s))
-    for s in ZC_ORDER:
-        greet(zcs(*s))
-    for k in NEAR_D:
+    for k in (1, 2, 3):
+        greet(xy(0, k))
+        greet(xy(k, 0))
+    for z in ZC_NEAR:
+        greet(zcs(*z))
+    for k in (4, -4, 8, -8):
         greet(linear(k))
-    for owner in owners:
-        @pl.when(owner != g)
-        def _():
-            greet((owner, q))
-    pl.semaphore_wait(barrier, 15 + 15 + len(NEAR_D) + count - own_inside)
+    ld_ut.wait()
+    for a in range(64):
+        ut[pl.ds(a, 126, stride=64), :] = utt[a].T
+    pl.semaphore_wait(barrier, 6 + len(ZC_NEAR) + 4)
+
+    def tell(semaphore, device):
+        pl.semaphore_signal(semaphore, inc=1, device_id=device, device_id_type=MESH)
 
     def remote(src, dst, ss, rs, device):
         c = pltpu.make_async_remote_copy(
@@ -143,8 +146,12 @@
         ins.append(
             remote(columns, vin.at[pl.ds(2 * q, 2), 8:24], in_send.at[k], in_recv.at[k], (g, lax.rem(q + k, 4)))
         )
-    sent.append(remote(columns.at[:, 8:16], vin.at[pl.ds(2 * q, 2), 0:8], edge_send.at[0], edge_recv.at[0, q], (group(1), 0)))
-    sent.append(remote(columns.at[:, 0:8], vin.at[pl.ds(2 * q, 2), 24:32], edge_send.at[1], edge_recv.at[1, q], (group(-1), 3)))
+    for k in (1, 2, 3):
+        tell(ready_xy, xy(k, 0))
+    for k in (2, 6):
+        tell(ready_z, zcs(k, 0))
+    for k in (1, -1):
+        tell(ready_group, (group(k), q))
 
     def by_offset(blocks, entries, number):
         found = []
@@ -162,20 +169,31 @@
     dsend[0] = low_half
     dsend[1] = high_half
 
-    def give(i, carry):
-        to = first_below + i
-
-        @pl.when(to != g)
-        def _():
-            remote(dsend, dbuf.at[level - 2], d_send.at[i], d_recv.at[level - 2], (to, q))
-
-        @pl.when(to == g)
-        def _():
-            pltpu.make_async_copy(dsend, dbuf.at[level - 2], d_recv.at[level - 2]).start()
-
-        return carry
-
-    lax.fori_loop(0, count, give, 0)
+    def matrix(n, many=1):
+        return ut[pl.ds(pl.multiple_of(64 * n, 64), 64 * many), :]
+
+    def pair(t, n):
+        return matrix(2**t - 2 + 2 * n, 2)
+
+    for n in range(16):
+        for m in range(2):
+            high, low = parts(mm(pair(6, 2 * n + m), matrix(2**5 - 2 + 2 * n + m), NN))
+            u_high[n, 128 * m : 128 * m + 128] = high
+            u_low[n, 128 * m : 128 * m + 128] = low
+    for n in range(4):
+        for m in range(2):
+            high, low = parts(mm(pair(4, 2 * n + m), matrix(2**3 - 2 + 2 * n + m), NN))
+            v_high[n, 128 * m : 128 * m + 128] = high
+            v_low[n, 128 * m : 128 * m + 128] = low
+    chain = {5: matrix(2**6 - 2 + g)}
+    for t in (4, 3, 2, 1, 0):
+        chain[t] = mm(chain[t + 1], matrix(2 ** (t + 1) - 2 + g // 2 ** (5 - t)), NN)
+    root_part = mm(jnp.zeros((8, 64), F32), chain[0], NT)
+    for t in range(2, 6):
+        gmap[t - 2, 2] = jnp.concatenate([chain[t], chain[t]], axis=1)
+    pl.semaphore_wait(ready_z, 2)
+    for k in (1, 2, 3):
+        tell(ready_plane, xy(k, 0))
 
     for c in ld_e:
         c.wait()
@@ -311,72 +329,60 @@
         z7 = coupled(k7, [middle_lists[1 + q // 2, k] for k in range(4)], pick7)
         return mm(z7, q7s[...], NT)
 
-    def upper_operator():
-        offsets = {2: 0, 3: 2, 4: 6, 5: 14, 6: 30}
-        lefts = left_lanes((64, 128))
-        ld_ut.wait()
-
-        def transfer(t):
-            return ut[2**t - 2 + g // 2 ** (6 - t)]
-
-        chain = {5: transfer(6)}
-        for t in (4, 3, 2, 1, 0):
-            chain[t] = mm(chain[t + 1], transfer(t + 1), NN)
-        ld_k[4].wait()
-
-        def add(t, lower, upper):
-            number = g // 2 ** (6 - t)
-            for j, offset in enumerate((-3, -2, 2, 3)):
-                at = jnp.clip(number + offset, 0, 2**t - 1)
-                block = lower if offset < 0 else upper
-                block = jnp.where(lax.rem(at, 2) == j % 2, block, swap(block))
-                kept = jnp.where(lefts == (lax.rem(at, 2) == 0), block, 0.0)
-                abuf[offsets[t] + at // 2] = abuf[offsets[t] + at // 2] + kept
-
-        abuf[0:2] = jnp.zeros((2, 64, 128), F32)
+    def upper_maps():
         for t in range(2, 6):
             pltpu.make_async_copy(dbuf.at[t - 2], dbuf.at[t - 2], d_recv.at[t - 2]).wait()
-            add(t, mm(chain[t], dbuf[t - 2, 0], NN), mm(chain[t], dbuf[t - 2, 1], NN))
-
-            def widen(i, carry):
-                tile = abuf[offsets[t] + i]
-                for half in range(2):
-                    x = tile[:, 0:64] if half == 0 else swap(tile)[:, 0:64]
-                    n = 2 * i + half
-                    e = ut[pl.ds(2 ** (t + 1) - 2 + 2 * n, 2)].reshape(128, 64)
-                    abuf[offsets[t + 1] + n] = mm(x, e, NT)
-                return carry
-
-            lax.fori_loop(0, 2 ** (t - 1), widen, 0, unroll=2)
-        add(6, *by_offset(k6, [middle_lists[0, k] for k in range(4)], g))
-
-        def keep(i, carry):
-            high, low = parts(abuf[30 + i])
-            ahigh[i] = high
-            alow[i] = low
-            return carry
-
-        lax.fori_loop(0, 32, keep, 0, unroll=4)
-        root = jnp.zeros((8, 64), F32)
-        return mm(root, chain[0], NT)
+            down = gmap[t - 2, 2][:, 0:64]
+            for half in range(2):
+                gmap[t - 2, half] = mm(down, dbuf[t - 2, half], NN)
+        ld_k[4].wait()
+        lower, upper = by_offset(k6, [middle_lists[0, k] for k in range(4)], g)
+        gmap[4, 0] = lower
+        gmap[4, 1] = upper
 
     def upper(p):
         for c in ags[p]:
             c.wait_recv()
         sent.extend(ags[p])
-        total = None
+        roots = []
         for x in range(2):
+            line = []
             for z in range(8):
                 zslot = lax.rem(gz - z + 8, 8)
                 even = agbuf[p, zslot, gc, x]
                 odd = agbuf[p, zslot, 1 - gc, x]
-                for h in range(2):
-                    both = jnp.where(left, even, swap(odd)) if h == 0 else jnp.where(left, swap(even), odd)
-                    i = (2 * x + h) * 8 + z
-                    xs = stacked(both)
-                    term = dot(xs, ahigh[i], NT) + dot(xs, alow[i], NT)
-                    total = term if total is None else total + term
-        return total[:8] + total[8:]
+                line.append((jnp.where(left, even, swap(odd)), jnp.where(left, swap(even), odd)))
+            roots.extend([a for a, b in line] + [b for a, b in line])
+        for i in range(32):
+            ctile[16 + i] = roots[i]
+        quads = []
+        for n in range(16):
+            x = jnp.concatenate([roots[2 * n], roots[2 * n + 1]], axis=1)
+            quads.append(mm_parts(stacked(x), u_high[n], u_low[n], NN))
+        fours = [jnp.concatenate([quads[2 * n], quads[2 * n + 1]], axis=1) for n in range(8)]
+        for n in range(8):
+            ctile[n] = fours[n]
+        total = root_part
+        for t in range(2, 7):
+            number = g // 2 ** (6 - t)
+            for half, offsets in enumerate(((-3, -2), (2, 3))):
+                found = []
+                for offset in offsets:
+                    n = jnp.clip(number + offset, 0, 2**t - 1)
+                    if t == 6:
+                        c = half_of(ctile[16 + n // 2], lax.rem(n, 2))
+                    elif t == 5:
+                        c = mm(ctile[16 + n], pair(6, n), NN)
+                    elif t == 4:
+                        c = half_of(ctile[n // 2], lax.rem(n, 2))
+                    elif t == 3:
+                        c = mm(ctile[n], pair(4, n), NN)
+                    else:
+                        x = jnp.concatenate([ctile[2 * n], ctile[2 * n + 1]], axis=1)
+                        c = mm_parts(stacked(x), v_high[n], v_low[n], NN)
+                    found.append(c)
+                total = total + mm(jnp.concatenate(found, axis=1), gmap[t - 2, half], NT)
+        return total
 
     def finish(p, base, w6):
         w10 = base + mm(w6, q6s[...], NT)
@@ -387,7 +393,28 @@
         return rows
 
     rows = jnp.concatenate([vlf[4 + 4 * q + l] for l in range(4)], axis=0)
+    pl.semaphore_wait(ready_xy, 3)
+    pl.semaphore_wait(ready_group, 2)
     climb(0, rows)
+    sent.append(remote(columns.at[:, 8:16], vin.at[pl.ds(2 * q, 2), 0:8], edge_send.at[0], edge_recv.at[0, q], (group(1), 0)))
+    sent.append(remote(columns.at[:, 0:8], vin.at[pl.ds(2 * q, 2), 24:32], edge_send.at[1], edge_recv.at[1, q], (group(-1), 3)))
+    pl.semaphore_wait(ready_plane, 3)
+
+    def give(i, carry):
+        to = first_below + i
+
+        @pl.when(to != g)
+        def _():
+            remote(dsend, dbuf.at[level - 2], d_send.at[i], d_recv.at[level - 2], (to, q))
+
+        @pl.when(to == g)
+        def _():
+            pltpu.make_async_copy(dsend, dbuf.at[level - 2], d_recv.at[level - 2]).start()
+
+        return carry
+
+    lax.fori_loop(0, count, give, 0)
+
 
     @pl.when(q == 0)
     def _():
@@ -410,9 +437,9 @@
     middle(0)
     for c in ld_k[:4]:
         c.wait()
-    root_part = upper_operator()
+    upper_maps()
     base = local_coupled(0) + middle_coupled(0)
-    first = finish(0, base, upper(0) + root_part)
+    first = finish(0, base, upper(0))
     for l in range(4):
         vnext[4 + l] = first[8 * l : 8 * l + 8]
     vs = [
@@ -429,7 +456,7 @@
     near_field(vnext, 4 * d - 4, 0)
     middle(1)
     base = local_coupled(1) + middle_coupled(1)
-    finish(1, base, upper(1) + root_part)
+    finish(1, base, upper(1))
     out1 = pltpu.make_async_copy(outs.at[1], second_hbm, out_sem.at[1])
     out1.start()
 
@@ -476,23 +503,26 @@
             vm(8, 32, 256), vm(24, 8, 256), vm(12, 8, 256), vm(32, 256, 256), vm(4, 64, 256),
             vm(4, 64, 64), vm(2, 64, 64), vm(64, 64), vm(64, 64),
             vm(4, 4, 64, 64), vm(2, 4, 64, 64), vm(4, 64, 64), vm(4, 64, 64), vm(4, 64, 64),
-            vm(126, 64, 64), vm(4, 64, 64),
-            vm(2, 64, 128), vm(4, 2, 64, 128), vm(62, 64, 128),
-            pltpu.VMEM((32, 64, 128), BF16), pltpu.VMEM((32, 64, 128), BF16),
+            vm(64, 64, 126), vm(126 * 64, 64), vm(4, 64, 64),
+            vm(2, 64, 128), vm(4, 2, 64, 128),
+            pltpu.VMEM((16, 256, 64), BF16), pltpu.VMEM((16, 256, 64), BF16),
+            pltpu.VMEM((4, 256, 64), BF16), pltpu.VMEM((4, 256, 64), BF16),
+            vm(5, 3, 64, 128), vm(48, 8, 128),
             vm(256, 256), vm(256, 64), vm(256, 64), vm(256, 64),
             vm(7, 4, 8, 128), vm(7, 4, 8, 128), vm(2, 4, 4, 8, 128), vm(2, 2, 8, 128), vm(2, 8, 2, 2, 8, 128),
             vm(5, 8, 128), vm(5, 8, 128), vm(32, 256), vm(2, 4, 8, 256),
             dma(16), dma(4), dma(4), dma(2), dma(2, 4), dma(16), dma(4),
             dma(2, 4, 4), dma(2, 4, 4), dma(2, 7), dma(2, 7), dma(2, 8, 2), dma(2, 8, 2),
             dma(2, 5), dma(2, 5), dma(2), dma(2), dma(2),
+            *[pltpu.SemaphoreType.REGULAR] * 4,
         ],
         compiler_params=pltpu.CompilerParams(
-            collective_id=0, has_side_effects=True, vmem_limit_bytes=48 * 2**20
+            collective_id=0, has_side_effects=True, vmem_limit_bytes=62 * 2**20
         ),
     )(
         near_pairs.T, local_lists.T, middle_lists, upper_lists,
         input_columns, near_blocks, leaf_basis, local_transfer, local_coupling,
-        middle_transfer, middle_coupling, upper_transfer, upper_coupling,
+        middle_transfer, middle_coupling, upper_transfer.transpose(1, 2, 0), upper_coupling,
     )
     return (first.transpose(1, 0, 2), second.transpose(1, 0, 2))
 

time: 73.8 us -> 64.4 us (0.87)
  local copies, waits for them, and re-layouts: 9.02 us -> 2.77 us
  Pallas kernels: 63.9 us -> 60.7 us
    unnamed x25 -> x2, local copies, waits for them, and re-layouts: 9.02 us -> 2.77 us
    pallas_call x1, Pallas kernels: 63.9 us -> 60.7 us  [body(): pl.pallas_call(kernel, out_shape=[jax.ShapeDtypeStruct((4, 8, 256), F32)]...]
where the time goes in v2:
time: 64.4 us; the launch traced here: 64.1 us
  Pallas kernels  60.7 us (94%)
  local copies, waits for them, and re-layouts  2.77 us (4%)
    pallas_call x1, Pallas kernels, body(): pl.pallas_call(kernel, out_shape=[jax.ShapeDtypeStruct((4, 8, 256), F32)]...  60.7 us
    unnamed x2, local copies, waits for them, and re-layouts  2.77 us

profile of v2, /device:TPU:1, one launch (start us, length us, event | category | flops | bytes accessed | tf_op | source)
XLA Modules:
  0.0 64.1 jit_solution(7314830240099095765)
XLA Ops:
  0.6 60.7 %shard_map.140 = (f32[4,8,256]{2,1,0:T(8,128)}, f32[4,8,256]{2,1,0:T(8,128)}) custom-call(s32[2,32]{1,0:T(2,128)} %bitcast.9, s32[4,28]{1,0:T(4,128)} %bitcast.8, s32[3,4]{1,0:T(4,128)} %middle_lists.1, s32[1,4]{1,0:T(1,128)} %upper_lists.1, f32[2,16,256]{2,1,0:T(8,128)} %columns.1, f32[32,256,256]{2,1,0:T(8,128)} %near_hbm.1, f32[4,64,256]{2,1,0:T(8,128)} %basis_hbm.1, ...), custom_call_target="tpu_custom_call" | custom-call | tf_op jit(solution)/shard_map/pallas_call | solution.py:497
  61.3 1.4 %copy.15 = f32[8,4,256]{2,1,0:T(4,128)} copy(f32[8,4,256]{2,0,1:T(8,128)} %bitcast.7) | data formatting | bytes 65536
  62.7 1.4 %copy.16 = f32[8,4,256]{2,1,0:T(4,128)} copy(f32[8,4,256]{2,0,1:T(8,128)} %bitcast.6) | data formatting | bytes 65536

commit v3 on v2

--- a/solution.py
+++ b/solution.py
@@ -57,7 +57,7 @@
     halo_0, halo_1, xybuf, agsend, agbuf, c7_0, c7_1, acc, outs,
     load_sem, in_send, in_recv, edge_send, edge_recv, d_send, d_recv,
     xy_send, xy_recv, halo_send, halo_recv, ag_send, ag_recv, c7_send, c7_recv, v_send, v_recv, out_sem,
-    ready_xy, ready_z, ready_group, ready_plane,
+    share_send, share_recv, ready_xy, ready_z, ready_group, ready_plane,
 ):
     halo, c7buf = (halo_0, halo_1), (c7_0, c7_1)
     g = lax.axis_index("leaf")
@@ -165,7 +165,10 @@
         return (jnp.concatenate(found[:2], axis=1), jnp.concatenate(found[2:], axis=1))
 
     ld_uc.wait()
-    low_half, high_half = by_offset(uc, [upper_lists[0, k] for k in range(4)], own_number)
+    quarter_rows = pl.ds(pl.multiple_of(16 * q, 16), 16)
+    low_half, high_half = by_offset(
+        [uc[k, quarter_rows, :] for k in range(4)], [upper_lists[0, k] for k in range(4)], own_number
+    )
     dsend[0] = low_half
     dsend[1] = high_half
 
@@ -329,12 +332,24 @@
         z7 = coupled(k7, [middle_lists[1 + q // 2, k] for k in range(4)], pick7)
         return mm(z7, q7s[...], NT)
 
-    def upper_maps():
+    def share_coupling():
+        shares = []
         for t in range(2, 6):
-            pltpu.make_async_copy(dbuf.at[t - 2], dbuf.at[t - 2], d_recv.at[t - 2]).wait()
+            view = dbuf.at[q, t - 2]
+            pltpu.make_async_copy(view, view, d_recv.at[t - 2]).wait()
+        for k in (2, 1, 3):
+            shares.append(remote(dbuf.at[q], dbuf.at[q], share_send.at[k], share_recv.at[k], xy(0, k)))
+        return shares
+
+    def upper_maps(shares):
+        for c in shares:
+            c.wait_recv()
+        sent.extend(shares)
+        for t in range(2, 6):
             down = gmap[t - 2, 2][:, 0:64]
             for half in range(2):
-                gmap[t - 2, half] = mm(down, dbuf[t - 2, half], NN)
+                block = jnp.concatenate([dbuf[k, t - 2, half] for k in range(4)], axis=0)
+                gmap[t - 2, half] = mm(down, block, NN)
         ld_k[4].wait()
         lower, upper = by_offset(k6, [middle_lists[0, k] for k in range(4)], g)
         gmap[4, 0] = lower
@@ -405,11 +420,11 @@
 
         @pl.when(to != g)
         def _():
-            remote(dsend, dbuf.at[level - 2], d_send.at[i], d_recv.at[level - 2], (to, q))
+            remote(dsend, dbuf.at[q, level - 2], d_send.at[i], d_recv.at[level - 2], (to, q))
 
         @pl.when(to == g)
         def _():
-            pltpu.make_async_copy(dsend, dbuf.at[level - 2], d_recv.at[level - 2]).start()
+            pltpu.make_async_copy(dsend, dbuf.at[q, level - 2], d_recv.at[level - 2]).start()
 
         return carry
 
@@ -435,10 +450,11 @@
     ld_near.wait()
     near_field(vlf, 16 * g - 4, 4 * q)
     middle(0)
+    shares = share_coupling()
     for c in ld_k[:4]:
         c.wait()
-    upper_maps()
     base = local_coupled(0) + middle_coupled(0)
+    upper_maps(shares)
     first = finish(0, base, upper(0))
     for l in range(4):
         vnext[4 + l] = first[8 * l : 8 * l + 8]
@@ -504,7 +520,7 @@
             vm(4, 64, 64), vm(2, 64, 64), vm(64, 64), vm(64, 64),
             vm(4, 4, 64, 64), vm(2, 4, 64, 64), vm(4, 64, 64), vm(4, 64, 64), vm(4, 64, 64),
             vm(64, 64, 126), vm(126 * 64, 64), vm(4, 64, 64),
-            vm(2, 64, 128), vm(4, 2, 64, 128),
+            vm(2, 16, 128), vm(4, 4, 2, 16, 128),
             pltpu.VMEM((16, 256, 64), BF16), pltpu.VMEM((16, 256, 64), BF16),
             pltpu.VMEM((4, 256, 64), BF16), pltpu.VMEM((4, 256, 64), BF16),
             vm(5, 3, 64, 128), vm(48, 8, 128),
@@ -514,7 +530,7 @@
             dma(16), dma(4), dma(4), dma(2), dma(2, 4), dma(16), dma(4),
             dma(2, 4, 4), dma(2, 4, 4), dma(2, 7), dma(2, 7), dma(2, 8, 2), dma(2, 8, 2),
             dma(2, 5), dma(2, 5), dma(2), dma(2), dma(2),
-            *[pltpu.SemaphoreType.REGULAR] * 4,
+            dma(4), dma(4), *[pltpu.SemaphoreType.REGULAR] * 4,
         ],
         compiler_params=pltpu.CompilerParams(
             collective_id=0, has_side_effects=True, vmem_limit_bytes=62 * 2**20

time: 64.4 us -> 55.5 us (0.86)
  Pallas kernels: 60.7 us -> 51.8 us
    pallas_call x1, Pallas kernels: 60.7 us -> 51.8 us  [body(): pl.pallas_call(kernel, out_shape=[jax.ShapeDtypeStruct((4, 8, 256), F32)]...]
where the time goes in v3:
time: 55.5 us; the launch traced here: 55.2 us
  Pallas kernels  51.8 us (93%)
  local copies, waits for them, and re-layouts  2.77 us (5%)
  between operations  0.64 us (1%)
    pallas_call x1, Pallas kernels, body(): pl.pallas_call(kernel, out_shape=[jax.ShapeDtypeStruct((4, 8, 256), F32)]...  51.8 us
    unnamed x2, local copies, waits for them, and re-layouts  2.77 us

profile of v3, /device:TPU:1, one launch (start us, length us, event | category | flops | bytes accessed | tf_op | source)
XLA Modules:
  0.0 55.2 jit_solution(14373928896355112135)
XLA Ops:
  0.6 51.8 %shard_map.140 = (f32[4,8,256]{2,1,0:T(8,128)}, f32[4,8,256]{2,1,0:T(8,128)}) custom-call(s32[2,32]{1,0:T(2,128)} %bitcast.9, s32[4,28]{1,0:T(4,128)} %bitcast.8, s32[3,4]{1,0:T(4,128)} %middle_lists.1, s32[1,4]{1,0:T(1,128)} %upper_lists.1, f32[2,16,256]{2,1,0:T(8,128)} %columns.1, f32[32,256,256]{2,1,0:T(8,128)} %near_hbm.1, f32[4,64,256]{2,1,0:T(8,128)} %basis_hbm.1, ...), custom_call_target="tpu_custom_call" | custom-call | tf_op jit(solution)/shard_map/pallas_call | solution.py:513
  52.5 1.4 %copy.15 = f32[8,4,256]{2,1,0:T(4,128)} copy(f32[8,4,256]{2,0,1:T(8,128)} %bitcast.7) | data formatting | bytes 65536
  53.8 1.4 %copy.16 = f32[8,4,256]{2,1,0:T(4,128)} copy(f32[8,4,256]{2,0,1:T(8,128)} %bitcast.6) | data formatting | bytes 65536

commit v4 on v3

--- a/solution.py
+++ b/solution.py
@@ -49,7 +49,7 @@
 
 
 def kernel(
-    pairs, local_lists, middle_lists, upper_lists,
+    pairs_hbm, local_hbm, middle_hbm, upper_hbm,
     columns, near_hbm, basis_hbm, lt_hbm, lc_hbm, mt_hbm, mc_hbm, ut_hbm, uc_hbm,
     first_hbm, second_hbm,
     vin, vlf, vnext, near, basis, e10, e9, e8, e7, k10, k9, k8, k7, k6, utt, ut, uc,
@@ -57,6 +57,7 @@
     halo_0, halo_1, xybuf, agsend, agbuf, c7_0, c7_1, acc, outs,
     load_sem, in_send, in_recv, edge_send, edge_recv, d_send, d_recv,
     xy_send, xy_recv, halo_send, halo_recv, ag_send, ag_recv, c7_send, c7_recv, v_send, v_recv, out_sem,
+    pairs, local_lists, middle_lists, upper_lists,
     share_send, share_recv, ready_xy, ready_z, ready_group, ready_plane,
 ):
     halo, c7buf = (halo_0, halo_1), (c7_0, c7_1)
@@ -80,6 +81,32 @@
     def zcs(i, k):
         return (gx * 16 + lax.rem(gz + i, 8) * 2 + lax.rem(gc + k, 2), q)
 
+    level = 2 + (g >= 8).astype(jnp.int32) + (g >= 16).astype(jnp.int32) + (g >= 32).astype(jnp.int32)
+    count = jnp.where(g >= 32, 2, jnp.where(g >= 16, 4, jnp.where(g >= 8, 8, jnp.where(g >= 4, 16, 0))))
+    start = jnp.where(g >= 32, 32, jnp.where(g >= 16, 16, jnp.where(g >= 8, 8, 4)))
+    own_number = g - start
+    first_below = own_number * count
+    own_inside = jnp.where((g >= first_below) & (g < first_below + count), 1, 0)
+    barrier = pltpu.get_barrier_semaphore()
+
+    def greet(device):
+        pl.semaphore_signal(barrier, inc=1, device_id=device, device_id_type=MESH)
+
+    for k in (1, 2, 3):
+        greet(xy(0, k))
+        greet(xy(k, 0))
+    for z in ZC_NEAR:
+        greet(zcs(*z))
+    past = jnp.where(gz == 7, 1 + gc, 0) + jnp.where(gz == 0, 2 - gc, 0)
+    for end, core, step in ((7, 1, 1), (0, 0, -1)):
+        @pl.when(gz == end)
+        def _():
+            greet((group(2 * step), q))
+
+        @pl.when((gz == end) & (gc == core))
+        def _():
+            greet((group(step), q))
+
     loads = []
 
     def load(src, dst):
@@ -90,6 +117,12 @@
 
     ld_own = load(columns, vin.at[pl.ds(2 * q, 2), 8:24])
     ld_ut = load(ut_hbm, utt)
+    ld_lists = [
+        load(upper_hbm, upper_lists),
+        load(middle_hbm, middle_lists),
+        load(local_hbm, local_lists),
+        load(pairs_hbm, pairs),
+    ]
     ld_e = [
         load(lt_hbm.at[pl.ds(12 + 4 * q, 4)], e10),
         load(lt_hbm.at[pl.ds(4 + 2 * q, 2)], e9),
@@ -107,28 +140,7 @@
     ]
     ld_near = load(near_hbm, near)
 
-    level = 2 + (g >= 8).astype(jnp.int32) + (g >= 16).astype(jnp.int32) + (g >= 32).astype(jnp.int32)
-    count = jnp.where(g >= 32, 2, jnp.where(g >= 16, 4, jnp.where(g >= 8, 8, jnp.where(g >= 4, 16, 0))))
-    start = jnp.where(g >= 32, 32, jnp.where(g >= 16, 16, jnp.where(g >= 8, 8, 4)))
-    own_number = g - start
-    first_below = own_number * count
-    own_inside = jnp.where((g >= first_below) & (g < first_below + count), 1, 0)
-    barrier = pltpu.get_barrier_semaphore()
-
-    def greet(device):
-        pl.semaphore_signal(barrier, inc=1, device_id=device, device_id_type=MESH)
-
-    for k in (1, 2, 3):
-        greet(xy(0, k))
-        greet(xy(k, 0))
-    for z in ZC_NEAR:
-        greet(zcs(*z))
-    for k in (4, -4, 8, -8):
-        greet(linear(k))
-    ld_ut.wait()
-    for a in range(64):
-        ut[pl.ds(a, 126, stride=64), :] = utt[a].T
-    pl.semaphore_wait(barrier, 6 + len(ZC_NEAR) + 4)
+    pl.semaphore_wait(barrier, 6 + len(ZC_NEAR) + past)
 
     def tell(semaphore, device):
         pl.semaphore_signal(semaphore, inc=1, device_id=device, device_id_type=MESH)
@@ -141,11 +153,18 @@
         return c
 
     sent = []
+    def give_half(k, half):
+        return remote(
+            columns.at[:, pl.ds(pl.multiple_of(8 * half, 8), 8)],
+            vin.at[pl.ds(2 * q, 2), pl.ds(pl.multiple_of(8 + 8 * half, 8), 8)],
+            in_send.at[late, k], in_recv.at[late, k], (g, lax.rem(q + k, 4)),
+        )
+
     ins = []
-    for k in (2, 1, 3):
-        ins.append(
-            remote(columns, vin.at[pl.ds(2 * q, 2), 8:24], in_send.at[k], in_recv.at[k], (g, lax.rem(q + k, 4)))
-        )
+    for late in range(2):
+        for k in (2, 1, 3):
+            half = lax.rem(q + k, 4) // 2
+            ins.append(give_half(k, half if late == 0 else 1 - half))
     for k in (1, 2, 3):
         tell(ready_xy, xy(k, 0))
     for k in (2, 6):
@@ -164,6 +183,11 @@
             found.append(total)
         return (jnp.concatenate(found[:2], axis=1), jnp.concatenate(found[2:], axis=1))
 
+    ld_ut.wait()
+    for a in range(64):
+        ut[pl.ds(a, 126, stride=64), :] = utt[a].T
+    for c in ld_lists:
+        c.wait()
     ld_uc.wait()
     quarter_rows = pl.ds(pl.multiple_of(16 * q, 16), 16)
     low_half, high_half = by_offset(
@@ -213,11 +237,16 @@
     quarter = lax.broadcasted_iota(jnp.int32, (8, 256), 1) // 64
     ld_own.wait()
     ld_basis.wait()
-    for c in ins:
+    for c in ins[:3]:
         c.wait_recv()
     sent.extend(ins)
-    for i in range(16):
-        vlf[4 + i] = vin[:, 8 + i, :]
+
+    def turn(half):
+        leaves = vin[:, pl.ds(pl.multiple_of(8 + 8 * half, 8), 8), :]
+        for i in range(8):
+            vlf[4 + 8 * half + i] = leaves[:, i, :]
+
+    turn(q // 2)
 
     def climb(p, rows):
         wide = mm(rows, basis[...].reshape(256, 256), NT)
@@ -447,6 +476,9 @@
         for i in range(4):
             vlf[20 + i] = vin[:, 24 + i, :]
 
+    for c in ins[3:]:
+        c.wait_recv()
+    turn(1 - q // 2)
     ld_near.wait()
     near_field(vlf, 16 * g - 4, 4 * q)
     middle(0)
@@ -506,14 +538,13 @@
     upper_coupling,
     upper_lists,
 ):
-    smem = pl.BlockSpec(memory_space=pltpu.SMEM)
     anywhere = pl.BlockSpec(memory_space=pl.ANY)
     vm = lambda *shape: pltpu.VMEM(shape, F32)
     dma = lambda *shape: pltpu.SemaphoreType.DMA(shape)
     first, second = pl.pallas_call(
         kernel,
         out_shape=[jax.ShapeDtypeStruct((4, 8, 256), F32)] * 2,
-        in_specs=[smem] * 4 + [anywhere] * 9,
+        in_specs=[anywhere] * 13,
         out_specs=[anywhere] * 2,
         scratch_shapes=[
             vm(8, 32, 256), vm(24, 8, 256), vm(12, 8, 256), vm(32, 256, 256), vm(4, 64, 256),
@@ -527,9 +558,11 @@
             vm(256, 256), vm(256, 64), vm(256, 64), vm(256, 64),
             vm(7, 4, 8, 128), vm(7, 4, 8, 128), vm(2, 4, 4, 8, 128), vm(2, 2, 8, 128), vm(2, 8, 2, 2, 8, 128),
             vm(5, 8, 128), vm(5, 8, 128), vm(32, 256), vm(2, 4, 8, 256),
-            dma(16), dma(4), dma(4), dma(2), dma(2, 4), dma(16), dma(4),
+            dma(20), dma(2, 4), dma(2, 4), dma(2), dma(2, 4), dma(16), dma(4),
             dma(2, 4, 4), dma(2, 4, 4), dma(2, 7), dma(2, 7), dma(2, 8, 2), dma(2, 8, 2),
             dma(2, 5), dma(2, 5), dma(2), dma(2), dma(2),
+            pltpu.SMEM((2, 32), jnp.int32), pltpu.SMEM((4, 28), jnp.int32),
+            pltpu.SMEM((3, 4), jnp.int32), pltpu.SMEM((1, 4), jnp.int32),
             dma(4), dma(4), *[pltpu.SemaphoreType.REGULAR] * 4,
         ],
         compiler_params=pltpu.CompilerParams(

time: 55.5 us -> 55.5 us (level)
  no operation moved by 1% of the time
where the time goes in v4:
time: 55.5 us; the launch traced here: 55.3 us
  Pallas kernels  51.9 us (94%)
  local copies, waits for them, and re-layouts  2.77 us (5%)
  between operations  0.64 us (1%)
    pallas_call x1, Pallas kernels, body(): pl.pallas_call(kernel, out_shape=[jax.ShapeDtypeStruct((4, 8, 256), F32)]...  51.9 us
    unnamed x2, local copies, waits for them, and re-layouts  2.77 us

profile of v4, /device:TPU:1, one launch (start us, length us, event | category | flops | bytes accessed | tf_op | source)
XLA Modules:
  0.0 55.3 jit_solution(14167752798183250411)
XLA Ops:
  0.6 51.9 %shard_map.140 = (f32[4,8,256]{2,1,0:T(8,128)}, f32[4,8,256]{2,1,0:T(8,128)}) custom-call(s32[2,32]{1,0:T(2,128)} %bitcast.9, s32[4,28]{1,0:T(4,128)} %bitcast.8, s32[3,4]{1,0:T(4,128)} %middle_hbm.1, s32[1,4]{1,0:T(1,128)} %upper_hbm.1, f32[2,16,256]{2,1,0:T(8,128)} %columns.1, f32[32,256,256]{2,1,0:T(8,128)} %near_hbm.1, f32[4,64,256]{2,1,0:T(8,128)} %basis_hbm.1, ...), custom_call_target="tpu_custom_call" | custom-call | tf_op jit(solution)/shard_map/pallas_call | solution.py:544
  52.5 1.4 %copy.15 = f32[8,4,256]{2,1,0:T(4,128)} copy(f32[8,4,256]{2,0,1:T(8,128)} %bitcast.7) | data formatting | bytes 65536
  53.9 1.4 %copy.16 = f32[8,4,256]{2,1,0:T(4,128)} copy(f32[8,4,256]{2,0,1:T(8,128)} %bitcast.6) | data formatting | bytes 65536

commit v5 on v4

--- a/solution.py
+++ b/solution.py
@@ -183,9 +183,6 @@
             found.append(total)
         return (jnp.concatenate(found[:2], axis=1), jnp.concatenate(found[2:], axis=1))
 
-    ld_ut.wait()
-    for a in range(64):
-        ut[pl.ds(a, 126, stride=64), :] = utt[a].T
     for c in ld_lists:
         c.wait()
     ld_uc.wait()
@@ -196,28 +193,6 @@
     dsend[0] = low_half
     dsend[1] = high_half
 
-    def matrix(n, many=1):
-        return ut[pl.ds(pl.multiple_of(64 * n, 64), 64 * many), :]
-
-    def pair(t, n):
-        return matrix(2**t - 2 + 2 * n, 2)
-
-    for n in range(16):
-        for m in range(2):
-            high, low = parts(mm(pair(6, 2 * n + m), matrix(2**5 - 2 + 2 * n + m), NN))
-            u_high[n, 128 * m : 128 * m + 128] = high
-            u_low[n, 128 * m : 128 * m + 128] = low
-    for n in range(4):
-        for m in range(2):
-            high, low = parts(mm(pair(4, 2 * n + m), matrix(2**3 - 2 + 2 * n + m), NN))
-            v_high[n, 128 * m : 128 * m + 128] = high
-            v_low[n, 128 * m : 128 * m + 128] = low
-    chain = {5: matrix(2**6 - 2 + g)}
-    for t in (4, 3, 2, 1, 0):
-        chain[t] = mm(chain[t + 1], matrix(2 ** (t + 1) - 2 + g // 2 ** (5 - t)), NN)
-    root_part = mm(jnp.zeros((8, 64), F32), chain[0], NT)
-    for t in range(2, 6):
-        gmap[t - 2, 2] = jnp.concatenate([chain[t], chain[t]], axis=1)
     pl.semaphore_wait(ready_z, 2)
     for k in (1, 2, 3):
         tell(ready_plane, xy(k, 0))
@@ -460,6 +435,31 @@
     lax.fori_loop(0, count, give, 0)
 
 
+    ld_ut.wait()
+    for a in range(64):
+        ut[pl.ds(a, 126, stride=64), :] = utt[a].T
+    def matrix(n, many=1):
+        return ut[pl.ds(pl.multiple_of(64 * n, 64), 64 * many), :]
+
+    def pair(t, n):
+        return matrix(2**t - 2 + 2 * n, 2)
+
+    for n in range(16):
+        for m in range(2):
+            high, low = parts(mm(pair(6, 2 * n + m), matrix(2**5 - 2 + 2 * n + m), NN))
+            u_high[n, 128 * m : 128 * m + 128] = high
+            u_low[n, 128 * m : 128 * m + 128] = low
+    for n in range(4):
+        for m in range(2):
+            high, low = parts(mm(pair(4, 2 * n + m), matrix(2**3 - 2 + 2 * n + m), NN))
+            v_high[n, 128 * m : 128 * m + 128] = high
+            v_low[n, 128 * m : 128 * m + 128] = low
+    chain = {5: matrix(2**6 - 2 + g)}
+    for t in (4, 3, 2, 1, 0):
+        chain[t] = mm(chain[t + 1], matrix(2 ** (t + 1) - 2 + g // 2 ** (5 - t)), NN)
+    root_part = mm(jnp.zeros((8, 64), F32), chain[0], NT)
+    for t in range(2, 6):
+        gmap[t - 2, 2] = jnp.concatenate([chain[t], chain[t]], axis=1)
     @pl.when(q == 0)
     def _():
         for k in range(4):
@@ -480,8 +480,8 @@
         c.wait_recv()
     turn(1 - q // 2)
     ld_near.wait()
+    middle(0)
     near_field(vlf, 16 * g - 4, 4 * q)
-    middle(0)
     shares = share_coupling()
     for c in ld_k[:4]:
         c.wait()

time: 55.5 us -> 52.4 us (0.944)
  Pallas kernels: 51.9 us -> 48.7 us
    pallas_call x1, Pallas kernels: 51.9 us -> 48.7 us  [body(): pl.pallas_call(kernel, out_shape=[jax.ShapeDtypeStruct((4, 8, 256), F32)]...]
where the time goes in v5:
time: 52.4 us; the launch traced here: 52.2 us
  Pallas kernels  48.7 us (93%)
  local copies, waits for them, and re-layouts  2.77 us (5%)
  between operations  0.64 us (1%)
    pallas_call x1, Pallas kernels, body(): pl.pallas_call(kernel, out_shape=[jax.ShapeDtypeStruct((4, 8, 256), F32)]...  48.7 us
    unnamed x2, local copies, waits for them, and re-layouts  2.77 us

profile of v5, /device:TPU:1, one launch (start us, length us, event | category | flops | bytes accessed | tf_op | source)
XLA Modules:
  0.0 52.2 jit_solution(12208653304549947801)
XLA Ops:
  0.6 48.7 %shard_map.140 = (f32[4,8,256]{2,1,0:T(8,128)}, f32[4,8,256]{2,1,0:T(8,128)}) custom-call(s32[2,32]{1,0:T(2,128)} %bitcast.9, s32[4,28]{1,0:T(4,128)} %bitcast.8, s32[3,4]{1,0:T(4,128)} %middle_hbm.1, s32[1,4]{1,0:T(1,128)} %upper_hbm.1, f32[2,16,256]{2,1,0:T(8,128)} %columns.1, f32[32,256,256]{2,1,0:T(8,128)} %near_hbm.1, f32[4,64,256]{2,1,0:T(8,128)} %basis_hbm.1, ...), custom_call_target="tpu_custom_call" | custom-call | tf_op jit(solution)/shard_map/pallas_call | solution.py:544
  49.4 1.4 %copy.15 = f32[8,4,256]{2,1,0:T(4,128)} copy(f32[8,4,256]{2,0,1:T(8,128)} %bitcast.7) | data formatting | bytes 65536
  50.8 1.4 %copy.16 = f32[8,4,256]{2,1,0:T(4,128)} copy(f32[8,4,256]{2,0,1:T(8,128)} %bitcast.6) | data formatting | bytes 65536
